TPU v7x, 512 devices: a whole 4x4x16 slice. The times are simulated.
512 devices in a mesh: blk: 128 (over y, z, core), grp: 4 (over x).
Axes of the slice: x: 4, y: 4, z: 16, core: 2. Of those that a mesh axis runs over, the one named last changes fastest.
Arguments:
- spectra: bfloat16 [32768, 4, 1002], P(('blk', 'grp')), may hold values from -6 to 6
- mid_bin: int32 [2, 32768, 64], P(None, ('blk', 'grp')), may hold values from 0 to 127, as said below
- off_bin: int32 [2, 32768, 64], P(None, ('blk', 'grp')), may hold values from 0 to 15
- owner_slot: int32 [2048], replicated, may hold values from 0 to 2047, each once
Outputs:
- stack: float32 [101, 2048], P(None, ('blk', 'grp'))
Inputs may be any that keep to these rules, and one draw needn't show every extreme that they name: owner_slot is a permutation of the bin numbers. `mid_bin`: some midpoint bins are named by no pair.
All inputs are finite; a program needn't handle non-finite values.
Results may differ from a plain program's by a relative error of at most 0.0041.
Values may be sent and summed in bfloat16 or wider, within the bound.
A program may use at most 64 MiB of HBM per device.

v0:
```python
import jax
import jax.numpy as jnp
from jax import lax
from jax.sharding import PartitionSpec as P

LAG = 50
NOFF = 16


def passed_along(value, axis, by):
    size = lax.axis_size(axis)
    return lax.ppermute(value, axis, [(i, (i + by) % size) for i in range(size)])


def make_kernel(nfreq, nwin):
    nlags = 2 * LAG + 1
    freq = jnp.arange(nfreq).astype(jnp.float32)
    lags = (jnp.arange(nlags) - LAG).astype(jnp.float32)
    angle = 2.0 * jnp.pi * freq[:, None] * lags[None, :] / (2 * (nfreq - 1))
    weight = jnp.where((freq == 0) | (freq == nfreq - 1), 1.0, 2.0) / jnp.sqrt(
        jnp.float32(nwin * nfreq)
    )
    cos_rows = (weight[:, None] * jnp.cos(angle)).astype(jnp.bfloat16)
    sin_rows = (-weight[:, None] * jnp.sin(angle)).astype(jnp.bfloat16)
    return jnp.concatenate([cos_rows, sin_rows], 0)


def cross_corr(own, other, kernel, nfreq):
    nchan = own.shape[0]
    nwin = own.shape[1]
    first = own.astype(jnp.float32)
    second = other.astype(jnp.float32)
    cross_re = jnp.zeros((nchan, nchan, nfreq), jnp.float32)
    cross_im = jnp.zeros((nchan, nchan, nfreq), jnp.float32)
    for window in range(nwin):
        real_a = first[:, None, window, :nfreq]
        imag_a = first[:, None, window, nfreq:]
        real_b = second[None, :, window, :nfreq]
        imag_b = second[None, :, window, nfreq:]
        cross_re = cross_re + (real_a * real_b + imag_a * imag_b)
        cross_im = cross_im + (imag_a * real_b - real_a * imag_b)
    joined = jnp.concatenate([cross_re, cross_im], -1).astype(jnp.bfloat16)
    joined = joined.reshape(nchan * nchan, 2 * nfreq)
    return jnp.dot(joined, kernel, preferred_element_type=jnp.float32)


def shards(spectra, mid_bin, off_bin, owner_slot):
    nchan = spectra.shape[0]
    nwin = spectra.shape[1]
    nfreq = spectra.shape[2] // 2
    nbins = owner_slot.shape[0]
    nblocks = lax.axis_size("blk")
    ngroups = lax.axis_size("grp")
    per_dev = nbins // (nblocks * ngroups)
    kernel = make_kernel(nfreq, nwin)
    first = passed_along(spectra, "blk", 1)
    second = passed_along(spectra, "blk", 2)
    sums = jnp.zeros((nbins, kernel.shape[1]), jnp.float32)
    counts = jnp.zeros((nbins,), jnp.float32)
    for rnd, other in enumerate((first, second)):
        corr = cross_corr(spectra, other, kernel, nfreq)
        pos = owner_slot[mid_bin[rnd] * NOFF + off_bin[rnd]].reshape(-1)
        sums = sums + jax.ops.segment_sum(corr, pos, nbins)
        counts = counts + jax.ops.segment_sum(jnp.ones((nchan * nchan,), jnp.float32), pos, nbins)
    lag_sums = sums.T
    lag_counts = counts[None, :]
    nlags = lag_sums.shape[0]
    moved_sums, moved_counts = (
        lax.all_to_all(lag_sums, "blk", split_axis=1, concat_axis=1, tiled=True),
        lax.all_to_all(lag_counts, "blk", split_axis=1, concat_axis=1, tiled=True),
    )
    owner_sums = moved_sums.reshape(nlags, nblocks, ngroups * per_dev).sum(1)
    owner_counts = moved_counts.reshape(1, nblocks, ngroups * per_dev).sum(1)
    total, number = (
        lax.psum_scatter(owner_sums, "grp", scatter_dimension=1, tiled=True),
        lax.psum_scatter(owner_counts, "grp", scatter_dimension=1, tiled=True),
    )
    return total / jnp.sqrt(jnp.maximum(number, 1.0))


def solution(mesh):
    in_specs = (
        P(("blk", "grp"), None, None),
        P(None, ("blk", "grp"), None),
        P(None, ("blk", "grp"), None),
        P(),
    )
    out_specs = P(None, ("blk", "grp"))
    return jax.shard_map(shards, mesh=mesh, in_specs=in_specs, out_specs=out_specs, check_vma=False)
```

profile of v0, /device:TPU:1, one launch (start us, length us, event | category | flops | bytes accessed | tf_op | source)
XLA Modules:
  0.0 273.1 jit_solution(11367326845329446959)
XLA Ops:
  0.0 1.2 copy_convert_fusion
  1.3 4.4 %collective-permute-start.1 = (bf16[64,4,1002]{2,0,1:T(8,128)(2,1)S(1)}, bf16[64,4,1002]{2,0,1:T(8,128)(2,1)S(1)}, u32[]{:S(2)}, u32[]{:S(2)}) collective-permute-start(bf16[64,4,1002]{2,0,1:T(8,128)(2,1)S(1)} %get-tuple-element.36), channel_id=1, source_target_pairs={{0,8},{4,12},{8,16},{12,20},{16,24},{20,28},{24,32},{28,36},{32,40... | collective-permute-start | bytes 1539080 | tf_op jit(solution)/shard_map/ppermute | solution.py:12
  5.6 4.4 %collective-permute-start = (bf16[64,4,1002]{2,0,1:T(8,128)(2,1)S(1)}, bf16[64,4,1002]{2,0,1:T(8,128)(2,1)S(1)}, u32[]{:S(2)}, u32[]{:S(2)}) collective-permute-start(bf16[64,4,1002]{2,0,1:T(8,128)(2,1)S(1)} %get-tuple-element.36), channel_id=1, source_target_pairs={{0,4},{4,8},{8,12},{12,16},{16,20},{20,24},{24,28},{28,32},{32,36}... | collective-permute-start | bytes 1539080 | tf_op jit(solution)/shard_map/ppermute | solution.py:12
  10.0 0.8 compare_select_fusion
  11.0 23.0 %gather_fusion.1 = s32[4096]{0:T(1024)S(1)} fusion(s32[2048]{0:T(1024)S(1)} %copy-done, s32[4096]{0:T(1024)S(1)} %broadcast_clamp_fusion), kind=kCustom, calls=%fused_computation.1 | custom fusion | bytes 49152 | tf_op jit(solution)/shard_map/gather | solution.py:62
  34.1 23.0 %gather_fusion = s32[4096]{0:T(1024)S(1)} fusion(s32[2048]{0:T(1024)S(1)} %copy-done, s32[4096]{0:T(1024)S(1)} %broadcast_clamp_fusion.1), kind=kCustom, calls=%fused_computation | custom fusion | bytes 49152 | tf_op jit(solution)/shard_map/gather | solution.py:62
  57.1 22.1 %scatter_custom_fusion.2 = f32[2048]{0:T(1024)S(1)} fusion(s32[4096]{0:T(1024)S(1)} %gather_fusion, f32[4096]{0:T(1024)S(1)} %broadcast.187, f32[]{:T(128)} %constant.11.clone.1), kind=kCustom, calls=%fused_computation.56 | custom fusion | flops 4096 | bytes 8196 | tf_op jit(solution)/shard_map/scatter-add | solution.py:64
  79.2 22.1 %scatter_custom_fusion.3 = f32[2048]{0:T(1024)S(1)} fusion(s32[4096]{0:T(1024)S(1)} %gather_fusion.1, f32[4096]{0:T(1024)S(1)} %broadcast.187, f32[]{:T(128)} %constant.11.clone.1), kind=kCustom, calls=%fused_computation.54 | custom fusion | flops 4096 | bytes 8196 | tf_op jit(solution)/shard_map/scatter-add | solution.py:64
  101.3 0.7 all_to_all.14
  102.0 17.4 %all-to-all-start.1 = ((f32[1,128,16]{2,0,1:T(1,128)}), f32[1,128,16]{2,0,1:T(1,128)S(1)}, u32[]{:S(2)}, u32[]{:S(2)}) async-start(f32[1,128,16]{2,0,1:T(1,128)} %bitcast.32), calls=%async_computation.1 | async-start | bytes 131072 | tf_op jit(solution)/shard_map/all_to_all | solution.py:70
  119.5 1.0 multiply_convert_fusion.1
  120.9 0.2 slice_bitcast_fusion.7
  121.5 8.7 %add_convert_fusion.1 = (bf16[64,64,501]{2,1,0:T(8,128)(2,1)S(1)}, bf16[64,64,501]{2,1,0:T(8,128)(2,1)S(1)}) fusion(f32[64,501]{1,0:T(8,128)S(1)} %get-tuple-element.12, f32[64,501]{1,0:T(8,128)S(1)} %get-tuple-element.13, f32[64,501]{1,0:T(8,128)S(1)} %get-tuple-element.14, f32[64,501]{1,0:T(8,128)S(1)} %get-tuple-element.15, ...), kind=kLoop, calls=%fused_computation.15 | loop fusion | flops 65667072 | bytes 10260480 | tf_op jit(solution)/shard_map/convert
  130.2 2.7 fusion.4
  132.9 8.7 %add_convert_fusion.3 = (bf16[64,64,501]{2,1,0:T(8,128)(2,1)S(1)}, bf16[64,64,501]{2,1,0:T(8,128)(2,1)S(1)}) fusion(f32[64,501]{1,0:T(8,128)S(1)} %get-tuple-element.28, f32[64,501]{1,0:T(8,128)S(1)} %get-tuple-element.20, f32[64,501]{1,0:T(8,128)S(1)} %get-tuple-element.29, f32[64,501]{1,0:T(8,128)S(1)} %get-tuple-element.21, ...), kind=kLoop, calls=%fused_computation.17 | loop fusion | flops 65667072 | bytes 10260480 | tf_op jit(solution)/shard_map/convert.2
  141.7 4.5 %fusion = f32[4096,101]{1,0:T(8,128)} fusion(bf16[4096,501]{1,0:T(8,128)(2,1)S(1)} %bitcast.71, bf16[4096,501]{1,0:T(8,128)(2,1)S(1)} %bitcast.70, bf16[501,101]{1,0:T(8,128)(2,1)S(1)} %get-tuple-element.40, bf16[501,101]{1,0:T(8,128)(2,1)S(1)} %get-tuple-element.39), kind=kOutput, calls=%fused_computation.6 | convolution fusion | flops 845868352 | bytes 10065572 | tf_op jit(solution)/shard_map/dot_general | solution.py:44
  146.1 22.8 %scatter_custom_fusion.1 = f32[2048,101]{1,0:T(8,128)S(1)} fusion(s32[4096]{0:T(1024)S(1)} %gather_fusion.1, f32[4096,101]{1,0:T(8,128)S(1)} %fusion.4, f32[]{:T(128)} %constant.11.clone.1), kind=kCustom, calls=%fused_computation.18 | custom fusion | flops 413696 | bytes 827396 | tf_op jit(solution)/shard_map/scatter-add | solution.py:63
  168.9 22.9 %scatter_custom_fusion = f32[2048,101]{1,0:T(8,128)S(1)} fusion(s32[4096]{0:T(1024)S(1)} %gather_fusion, f32[4096,101]{1,0:T(8,128)} %fusion, f32[]{:T(128)} %constant.11.clone.1), kind=kCustom, calls=%fused_computation.20 | custom fusion | flops 413696 | bytes 827904 | tf_op jit(solution)/shard_map/scatter-add | solution.py:63
  191.9 1.1 add.209
  193.0 16.2 %all-to-all-start = ((f32[101,128,16]{0,2,1:T(8,128)}), f32[101,128,16]{0,2,1:T(8,128)S(1)}, u32[]{:S(2)}, u32[]{:S(2)}) async-start(f32[101,128,16]{0,2,1:T(8,128)} %bitcast.31), calls=%async_computation | async-start | bytes 2097152 | tf_op jit(solution)/shard_map/all_to_all | solution.py:69
  209.2 1.3 dynamic-slice
  211.2 52.3 %all-to-all-done = f32[101,128,16]{0,2,1:T(8,128)S(1)} async-done(((f32[101,128,16]{0,2,1:T(8,128)}), f32[101,128,16]{0,2,1:T(8,128)S(1)}, u32[]{:S(2)}, u32[]{:S(2)}) %all-to-all-start) | async-done | bytes 827424 | tf_op jit(solution)/shard_map/all_to_all | solution.py:69
  263.7 8.7 %all-reduce.2 = (f32[101,16]{0,1:T(8,128)S(1)}, f32[1,16]{1,0:T(1,128)S(1)}) all-reduce(f32[101,16]{0,1:T(8,128)S(1)} %reduce_sum.20, f32[1,16]{1,0:T(1,128)S(1)} %bitcast.74), channel_id=2, replica_groups=mesh['blk'=128,'grp'=4] {'grp'}, use_global_device_ids=true, to_apply=%region_3.4.clone | all-reduce | flops 1632 | bytes 13056
  272.4 0.7 dynamic-slice_divide_fusion
  (21 shorter events, 1.2 us)
Async XLA Ops:
  0.0 11.0 %copy-start = (s32[2048]{0:T(1024)S(1)}, s32[2048]{0:T(1024)}, u32[]{:S(2)}) copy-start(s32[2048]{0:T(1024)} %param.7) | copy-start | bytes 24580
  1.3 119.5 %collective-permute-start.1 = (bf16[64,4,1002]{2,0,1:T(8,128)(2,1)S(1)}, bf16[64,4,1002]{2,0,1:T(8,128)(2,1)S(1)}, u32[]{:S(2)}, u32[]{:S(2)}) collective-permute-start(bf16[64,4,1002]{2,0,1:T(8,128)(2,1)S(1)} %get-tuple-element.36), channel_id=1, source_target_pairs={{0,8},{4,12},{8,16},{12,20},{16,24},{20,28},{24,32},{28,36},{32,40... | collective-permute-start | bytes 1539080 | tf_op jit(solution)/shard_map/ppermute | solution.py:12
  5.6 115.5 %collective-permute-start = (bf16[64,4,1002]{2,0,1:T(8,128)(2,1)S(1)}, bf16[64,4,1002]{2,0,1:T(8,128)(2,1)S(1)}, u32[]{:S(2)}, u32[]{:S(2)}) collective-permute-start(bf16[64,4,1002]{2,0,1:T(8,128)(2,1)S(1)} %get-tuple-element.36), channel_id=1, source_target_pairs={{0,4},{4,8},{8,12},{12,16},{16,20},{20,24},{24,28},{28,32},{32,36}... | collective-permute-start | bytes 1539080 | tf_op jit(solution)/shard_map/ppermute | solution.py:12
  102.0 90.9 %all-to-all-start.1 = ((f32[1,128,16]{2,0,1:T(1,128)}), f32[1,128,16]{2,0,1:T(1,128)S(1)}, u32[]{:S(2)}, u32[]{:S(2)}) async-start(f32[1,128,16]{2,0,1:T(1,128)} %bitcast.32), calls=%async_computation.1 | async-start | bytes 131072 | tf_op jit(solution)/shard_map/all_to_all | solution.py:70
  193.0 70.5 %all-to-all-start = ((f32[101,128,16]{0,2,1:T(8,128)}), f32[101,128,16]{0,2,1:T(8,128)S(1)}, u32[]{:S(2)}, u32[]{:S(2)}) async-start(f32[101,128,16]{0,2,1:T(8,128)} %bitcast.31), calls=%async_computation | async-start | bytes 2097152 | tf_op jit(solution)/shard_map/all_to_all | solution.py:69
where the time goes:
time: 276 us; the launch traced here: 273 us
  other arithmetic  113 us (41%)
  waiting for transfers between devices  52.3 us (19%)
  local copies, waits for them, and re-layouts  48.8 us (18%)
  starting transfers between devices  42.4 us (15%)
  blocking collectives  8.7 us (3%)
  matrix products  7.18 us (3%)
    all_to_all x1, waiting for transfers between devices, shards(): lax.all_to_all(lag_sums, 'blk', split_axis=1, concat_axis=1, tiled=True)  52.3 us
    gather x2, local copies, waits for them, and re-layouts, shards(): pos = owner_slot[mid_bin[rnd] * NOFF + off_bin[rnd]].reshape(-1)  46.1 us
    scatter-add x2, other arithmetic, shards(): sums = sums + jax.ops.segment_sum(corr, pos, nbins)  45.7 us
    scatter-add x2, other arithmetic, shards(): jax.ops.segment_sum(jnp.ones((nchan * nchan,), jnp.float32), pos, nbins)  44.2 us
    another operation x2, other arithmetic  17.5 us
    all_to_all x1, starting transfers between devices, shards(): lax.all_to_all(lag_counts, 'blk', split_axis=1, concat_axis=1, tiled=True)  17.4 us
    all_to_all x1, starting transfers between devices, shards(): lax.all_to_all(lag_sums, 'blk', split_axis=1, concat_axis=1, tiled=True)  16.2 us
    ppermute x2, starting transfers between devices, passed_along(): lax.ppermute(value, axis, [(i, (i + by) % size) for i in range(size)])  8.76 us
  transfers between devices with their start and end apart: 4, of which 1 were waited for; matrix products, arithmetic and copies ran while one was open for 61% of the time, Pallas kernels for 0%

commit v1 on v0

v1 whole, which is shorter than its diff:
```python
import jax
import jax.numpy as jnp
import numpy as np
from jax import lax
from jax.experimental import pallas as pl
from jax.experimental.pallas import tpu as pltpu
from jax.sharding import PartitionSpec as P

LAG=50; NOFF=16
F=501; W=4; FP=512; TL=128; NL=101

def lag_matrix():
    freq=np.arange(F,dtype=np.float32); lags=(np.arange(NL)-LAG).astype(np.float32)
    angle=(np.float32(2.0*np.pi)*freq[:,None]*lags[None,:]/np.float32(2*(F-1))).astype(np.float32)
    w=np.where((freq==0)|(freq==F-1),1.0,2.0).astype(np.float32)/np.sqrt(np.float32(W*F))
    k=np.zeros((2*FP,TL),np.float32)
    k[:F,:NL]=w[:,None]*np.cos(angle)
    k[FP:FP+F,:NL]=-w[:,None]*np.sin(angle)
    return jnp.asarray(k,jnp.bfloat16)

def prep(spectra):
    x=spectra.reshape(4,16,W,2,F).transpose(0,3,2,1,4)
    x=jnp.pad(x,((0,0),)*4+((0,FP-F),))
    return x.reshape(4,8,16,FP)

def prep_idx(mid,off):
    b=mid*NOFF+off
    return b.reshape(2,4,16,4,16).transpose(0,3,1,2,4).reshape(32,256)

def cross_tile(a_ref, b_ref, dst, ib, jcx):
    for ft in range(4):
        sl=pl.ds(ft*128,128)
        B=[b_ref[jcx,k,:,sl].astype(jnp.float32) for k in range(8)]
        for ii in range(16):
            A=[jnp.broadcast_to(a_ref[ib,k,pl.ds(ii,1),sl],(16,128)) for k in range(8)]
            re=None; im=None
            for w in range(4):
                r=A[w]*B[w]+A[4+w]*B[4+w]
                m=A[4+w]*B[w]-A[w]*B[4+w]
                re=r if re is None else re+r
                im=m if im is None else im+m
            dst[pl.ds(ii*16,16),pl.ds(ft*128,128)]=re.astype(jnp.bfloat16)
            dst[pl.ds(ii*16,16),pl.ds(512+ft*128,128)]=im.astype(jnp.bfloat16)

def corr_tile(src, kmat_ref, pos_ref, corrx, t):
    c=jnp.dot(src[...],kmat_ref[...],preferred_element_type=jnp.float32)
    lane=lax.broadcasted_iota(jnp.int32,(256,TL),1)
    c=jnp.where((lane==NL)|(lane==NL+1),1.0,c)
    bit=(pos_ref[pl.ds(t,1),:]&1).astype(jnp.float32)
    mask=jnp.transpose(jnp.broadcast_to(bit,(128,256)))
    hi=c*mask
    row=pl.multiple_of(t*256,256)
    corrx[pl.ds(row,256),pl.ds(0,TL)]=(c-hi).astype(jnp.bfloat16)
    corrx[pl.ds(row,256),pl.ds(TL,TL)]=hi.astype(jnp.bfloat16)

def lookup(bin_ref, tab_ref, pos_ref):
    tab=tab_ref[...]
    lo=(tab&255).astype(jnp.float32); hi=(tab>>8).astype(jnp.float32)
    tt=jnp.concatenate([lo,hi],0).astype(jnp.bfloat16)
    def body(t,_):
        b=bin_ref[pl.ds(t,1),:]
        sub=lax.broadcasted_iota(jnp.int32,(128,256),0)
        oh=jnp.where(sub==(b&127),1.0,0.0).astype(jnp.bfloat16)
        v=jnp.dot(tt,oh,preferred_element_type=jnp.float32)
        full=v[:16]+256.0*v[16:]
        s16=lax.broadcasted_iota(jnp.int32,(16,256),0)
        p=jnp.sum(jnp.where(s16==(b>>7),full,0.0),axis=0,keepdims=True)
        pos_ref[pl.ds(t,1),:]=p.astype(jnp.int32)
        return 0
    lax.fori_loop(0,32,body,0)

def make_onehot(pos_ref, oh_ref, base, rows):
    def body(t,_):
        a=(pos_ref[pl.ds(t,1),:]>>1)-base
        sub=lax.broadcasted_iota(jnp.int32,(rows,256),0)
        v=jnp.where(sub==a,1.0,0.0).astype(jnp.bfloat16)
        oh_ref[:,pl.ds(pl.multiple_of(t*256,256),256)]=v
        return 0
    lax.fori_loop(0,32,body,0)

def kernel(own_ref,oth_ref,bin_ref,tab_ref,kmat_ref,out_ref,a32,cA,cB,corrx,pos_ref,oh_ref):
    a32[...]=own_ref[...].astype(jnp.float32)
    lookup(bin_ref,tab_ref,pos_ref)
    def body(s,_):
        t=2*s
        rc=s//2
        ib=lax.rem(t,4)
        cross_tile(a32,oth_ref,cA,ib,rc)
        corr_tile(cB,kmat_ref,pos_ref,corrx,jnp.maximum(t-1,0))
        cross_tile(a32,oth_ref,cB,ib+1,rc)
        corr_tile(cA,kmat_ref,pos_ref,corrx,t)
        return 0
    lax.fori_loop(0,16,body,0)
    corr_tile(cB,kmat_ref,pos_ref,corrx,31)
    for h in range(2):
        make_onehot(pos_ref,oh_ref,h*512,512)
        out_ref[pl.ds(h*512,512),:]=jnp.dot(oh_ref[...],corrx[...],preferred_element_type=jnp.float32)

def run(own,oth,bins,tab,kmat):
    return pl.pallas_call(kernel,out_shape=jax.ShapeDtypeStruct((1024,256),jnp.float32),
        in_specs=[pl.BlockSpec(memory_space=pltpu.VMEM)]*5,out_specs=pl.BlockSpec(memory_space=pltpu.VMEM),
        scratch_shapes=[pltpu.VMEM((4,8,16,FP),jnp.float32),pltpu.VMEM((256,1024),jnp.bfloat16),pltpu.VMEM((256,1024),jnp.bfloat16),
            pltpu.VMEM((8192,256),jnp.bfloat16),pltpu.VMEM((32,256),jnp.int32),pltpu.VMEM((512,8192),jnp.bfloat16)],
        compiler_params=pltpu.CompilerParams(vmem_limit_bytes=60*2**20),
    )(own,oth,bins,tab,kmat)


def passed_along(value, axis, by):
    size = lax.axis_size(axis)
    return lax.ppermute(value, axis, [(i, (i + by) % size) for i in range(size)])


def shards(spectra, mid_bin, off_bin, owner_slot):
    own = prep(spectra)
    other = jnp.concatenate([passed_along(own, "blk", 1), passed_along(own, "blk", 2)], 0)
    table = owner_slot.reshape(16, 128)
    part = run(own, other, prep_idx(mid_bin, off_bin), table, lag_matrix())
    part = part.reshape(2048, TL)
    total = lax.psum_scatter(part, ("blk", "grp"), scatter_dimension=0, tiled=True)
    number = total[:, NL:NL + 1]
    return (total[:, :NL] / jnp.sqrt(jnp.maximum(number, 1.0))).T


def solution(mesh):
    in_specs = (
        P(("blk", "grp"), None, None),
        P(None, ("blk", "grp"), None),
        P(None, ("blk", "grp"), None),
        P(),
    )
    return jax.shard_map(shards, mesh=mesh, in_specs=in_specs, out_specs=P(None, ("blk", "grp")), check_vma=False)
```

time: 276 us -> 560 us (2.03)
  waiting for transfers between devices: 52.3 us -> 485 us
  other arithmetic: 113 us -> 1.97 us
  Pallas kernels: 0 us -> 44.3 us
  local copies, waits for them, and re-layouts: 48.8 us -> 5.65 us
  starting transfers between devices: 42.4 us -> 8.48 us
  between operations: 0.87 us -> 13.5 us
  blocking collectives: 8.7 us -> 0 us
  matrix products: 7.18 us -> 0 us
    unnamed x0 -> x2, waiting for transfers between devices: none -> 463 us
    scatter-add x4 -> x0, other arithmetic: 89.9 us -> none  [the longest x2 45.7 us: shards(): sums = sums + jax.ops.segment_sum(corr, pos, nbins)]
    all_to_all x2 -> x0, waiting for transfers between devices: 52.3 us -> none  [the longest x1 52.3 us: shards(): lax.all_to_all(lag_sums, 'blk', split_axis=1, concat_axis=1, tiled=True)]
    gather x2 -> x0, local copies, waits for them, and re-layouts: 46.1 us -> none  [shards(): pos = owner_slot[mid_bin[rnd] * NOFF + off_bin[rnd]].reshape(-1)]
    pallas_call x0 -> x1, Pallas kernels: none -> 44.3 us  [run(): pl.pallas_call(kernel, out_shape=jax.ShapeDtypeStruct((1024, 256), jnp.fl...]
    all_to_all x2 -> x0, starting transfers between devices: 33.6 us -> none  [the longest x1 17.4 us: shards(): lax.all_to_all(lag_counts, 'blk', split_axis=1, concat_axis=1, tiled=True)]
    ppermute x2, waiting for transfers between devices: 0.01 us -> 22.7 us  [passed_along(): lax.ppermute(value, axis, [(i, (i + by) % size) for i in range(size)])]
    another operation x2 -> x0, other arithmetic: 17.5 us -> none
  transfers between devices with their start and end apart: 4 -> 3, of which waited for: 1 -> 3; matrix products, arithmetic and copies ran while one was open for 61% -> 0% of each run, Pallas kernels for 0% -> 0%
where the time goes in v1:
time: 560 us; the launch traced here: 559 us
  waiting for transfers between devices  485 us (87%)
  Pallas kernels  44.3 us (8%)
  between operations  13.5 us (2%)
  starting transfers between devices  8.48 us (2%)
  local copies, waits for them, and re-layouts  5.65 us (1%)
    unnamed x2, waiting for transfers between devices  463 us
    pallas_call x1, Pallas kernels, run(): pl.pallas_call(kernel, out_shape=jax.ShapeDtypeStruct((1024, 256), jnp.fl...  44.3 us
    ppermute x2, waiting for transfers between devices, passed_along(): lax.ppermute(value, axis, [(i, (i + by) % size) for i in range(size)])  22.7 us
  transfers between devices with their start and end apart: 3, of which 3 were waited for; matrix products, arithmetic and copies ran while one was open for 0% of the time, Pallas kernels for 0%

profile of v1, /device:TPU:1, one launch (start us, length us, event | category | flops | bytes accessed | tf_op | source)
XLA Modules:
  0.0 559.4 jit_solution(18242841566306817820)
XLA Ops:
  6.5 0.0 all-reduce.4.cloned.1.call-start
  6.5 1.5 reshape.18
  8.0 0.2 copy.14
  8.2 0.0 copy-start.1
  8.2 0.0 copy-start.2
  8.2 0.1 pad.4
  8.3 0.0 copy-start
  8.3 4.9 collective-permute-start
  13.3 3.5 collective-permute-start.1
  16.8 0.0 copy-done.1
  16.8 0.0 copy-done.2
  16.8 0.2 reshape.20
  17.0 0.0 copy-done
  17.1 0.8 reshape.21.bin_ref
  17.8 1.6 collective-permute-done
  19.4 21.2 %collective-permute-done.1 = bf16[4,8,16,512]{3,2,1,0:T(8,128)(2,1)S(1)} collective-permute-done((bf16[4,8,16,512]{3,2,1,0:T(8,128)(2,1)S(1)}, bf16[4,8,16,512]{3,2,1,0:T(8,128)(2,1)S(1)}, u32[]{:S(2)}, u32[]{:S(2)}) %collective-permute-start.1) | collective-permute-done | bytes 524320 | tf_op jit(solution)/shard_map/ppermute | solution.py:110
  40.5 1.1 pad_maximum_fusion.oth_ref
  41.6 44.3 %shard_map.55 = f32[1024,256]{1,0:T(8,128)} custom-call(bf16[4,8,16,512]{3,2,1,0:T(8,128)(2,1)} %bitcast.15, bf16[8,8,16,512]{3,2,1,0:T(8,128)(2,1)} %pad_maximum_fusion.oth_ref, s32[32,256]{1,0:T(8,128)} %reshape.21.bin_ref, s32[16,128]{1,0:T(8,128)} %bitcast.17, bf16[1024,128]{1,0:T(8,128)(2,1)} %constant.9.clone.kmat_ref), custom_call_target="tpu_custom_call" | custom-call | tf_op jit(solution)/shard_map/pallas_call | solution.py:100
  85.9 2.3 reshape.23
  88.3 0.0 all-reduce.4.cloned.1.call-update
  88.3 462.7 %all-reduce.4.cloned.1.call-done = f32[2048,128]{1,0:T(8,128)} async-done(((f32[2048,128]{1,0:T(8,128)}), f32[2048,128]{1,0:T(8,128)}) %all-reduce.4.cloned.1.call-update) | async-done | bytes 1048592
  551.0 0.7 constant_dynamic-slice_fusion
  551.7 0.2 sqrt_reduce_fusion
  551.9 0.7 divide_bitcast_fusion
  (2 shorter events, 0.0 us)
Async XLA Ops:
  6.5 544.5 %all-reduce.4.cloned.1.call-start = ((), (), s32[]{:S(2)}) async-start(), calls=%async_computation | async-start | bytes 2097152
  8.2 8.6 %copy-start.1 = (s32[2,64,64]{2,1,0:T(8,128)S(1)}, s32[2,64,64]{2,1,0:T(8,128)}, u32[]{:S(2)}) copy-start(s32[2,64,64]{2,1,0:T(8,128)} %param.7) | copy-start | bytes 98308
  8.2 8.6 %copy-start.2 = (s32[2,64,64]{2,1,0:T(8,128)S(1)}, s32[2,64,64]{2,1,0:T(8,128)}, u32[]{:S(2)}) copy-start(s32[2,64,64]{2,1,0:T(8,128)} %param.6) | copy-start | bytes 98308
  8.3 8.7 %copy-start = (bf16[4,2,4,16,512]{4,3,2,1,0:T(8,128)(2,1)}, bf16[4,2,4,16,512]{4,3,2,1,0:T(8,128)(2,1)S(1)}, u32[]{:S(2)}) copy-start(bf16[4,2,4,16,512]{4,3,2,1,0:T(8,128)(2,1)S(1)} %pad.4) | copy-start | bytes 1572868
  8.3 11.0 %collective-permute-start = (bf16[4,8,16,512]{3,2,1,0:T(8,128)(2,1)S(1)}, bf16[4,8,16,512]{3,2,1,0:T(8,128)(2,1)S(1)}, u32[]{:S(2)}, u32[]{:S(2)}) collective-permute-start(bf16[4,8,16,512]{3,2,1,0:T(8,128)(2,1)S(1)} %bitcast.13), channel_id=1, source_target_pairs={{0,4},{4,8},{8,12},{12,16},{16,20},{20,24},{24,28},{28,32},{32,36}... | collective-permute-start | bytes 1572872 | tf_op jit(solution)/shard_map/ppermute | solution.py:110
  13.3 27.3 %collective-permute-start.1 = (bf16[4,8,16,512]{3,2,1,0:T(8,128)(2,1)S(1)}, bf16[4,8,16,512]{3,2,1,0:T(8,128)(2,1)S(1)}, u32[]{:S(2)}, u32[]{:S(2)}) collective-permute-start(bf16[4,8,16,512]{3,2,1,0:T(8,128)(2,1)S(1)} %bitcast.14), channel_id=1, source_target_pairs={{0,8},{4,12},{8,16},{12,20},{16,24},{20,28},{24,32},{28,36},{32,40... | collective-permute-start | bytes 1572872 | tf_op jit(solution)/shard_map/ppermute | solution.py:110
Sparse Core Ops, SparseCore 0:
  88.4 462.5 all-reduce.3

commit v2 on v1

--- a/solution.py
+++ b/solution.py
@@ -78,31 +78,158 @@
         return 0
     lax.fori_loop(0,32,body,0)
 
-def kernel(own_ref,oth_ref,bin_ref,tab_ref,kmat_ref,out_ref,a32,cA,cB,corrx,pos_ref,oh_ref):
-    a32[...]=own_ref[...].astype(jnp.float32)
-    lookup(bin_ref,tab_ref,pos_ref)
-    def body(s,_):
-        t=2*s
-        rc=s//2
-        ib=lax.rem(t,4)
-        cross_tile(a32,oth_ref,cA,ib,rc)
-        corr_tile(cB,kmat_ref,pos_ref,corrx,jnp.maximum(t-1,0))
-        cross_tile(a32,oth_ref,cB,ib+1,rc)
-        corr_tile(cA,kmat_ref,pos_ref,corrx,t)
-        return 0
-    lax.fori_loop(0,16,body,0)
-    corr_tile(cB,kmat_ref,pos_ref,corrx,31)
-    for h in range(2):
-        make_onehot(pos_ref,oh_ref,h*512,512)
-        out_ref[pl.ds(h*512,512),:]=jnp.dot(oh_ref[...],corrx[...],preferred_element_type=jnp.float32)
-
-def run(own,oth,bins,tab,kmat):
-    return pl.pallas_call(kernel,out_shape=jax.ShapeDtypeStruct((1024,256),jnp.float32),
-        in_specs=[pl.BlockSpec(memory_space=pltpu.VMEM)]*5,out_specs=pl.BlockSpec(memory_space=pltpu.VMEM),
-        scratch_shapes=[pltpu.VMEM((4,8,16,FP),jnp.float32),pltpu.VMEM((256,1024),jnp.bfloat16),pltpu.VMEM((256,1024),jnp.bfloat16),
-            pltpu.VMEM((8192,256),jnp.bfloat16),pltpu.VMEM((32,256),jnp.int32),pltpu.VMEM((512,8192),jnp.bfloat16)],
-        compiler_params=pltpu.CompilerParams(vmem_limit_bytes=60*2**20),
-    )(own,oth,bins,tab,kmat)
+
+NX, NY, NZ = 4, 4, 16
+MESH = pl.DeviceIdType.MESH
+
+
+def place():
+    blk = lax.axis_index("blk")
+    return lax.axis_index("grp"), blk // (2 * NZ), lax.rem(blk // 2, NZ), lax.rem(blk, 2)
+
+
+def device(x, y, z, core):
+    return {"blk": (y * NZ + z) * 2 + core, "grp": x}
+
+
+def plane_peer(d):
+    x, y, z, core = place()
+    return lax.rem(x + d // NY, NX), lax.rem(y + lax.rem(d, NY), NY), z, core
+
+
+def line_peer(d):
+    x, y, z, core = place()
+    return x, y, lax.rem(z + d, NZ), core
+
+
+def greet():
+    barrier = pltpu.get_barrier_semaphore()
+    x, y, z, core = place()
+    pl.semaphore_signal(barrier, inc=1, device_id=device(x, y, z, 1 - core), device_id_type=MESH)
+
+    def plane(d, _):
+        pl.semaphore_signal(barrier, inc=1, device_id=device(*plane_peer(d)), device_id_type=MESH)
+        return 0
+
+    def line(d, _):
+        pl.semaphore_signal(barrier, inc=1, device_id=device(*line_peer(d)), device_id_type=MESH)
+        return 0
+
+    lax.fori_loop(1, NX * NY, plane, 0)
+    lax.fori_loop(1, NZ, line, 0)
+
+
+def split_counts(v):
+    lane = lax.rem(lax.broadcasted_iota(jnp.int32, v.shape, len(v.shape) - 1), TL)
+    high = jnp.floor(v * (1.0 / 128.0)) * 128.0
+    return jnp.where(lane == NL, high, jnp.where(lane == NL + 1, v - high, v))
+
+
+def kernel(own_ref, oth_ref, bin_ref, tab_ref, kmat_ref, out_ref, a32, cA, cB, corrx, pos_ref, oh_ref,
+           away, came, keep, plane_out, plane_in, line_out, line_in,
+           core_sems, plane_send, plane_recv, line_send, line_recv):
+    greet()
+    a32[...] = own_ref[...].astype(jnp.float32)
+    lookup(bin_ref, tab_ref, pos_ref)
+
+    def body(s, _):
+        t = 2 * s
+        rc = s // 2
+        ib = lax.rem(t, 4)
+        cross_tile(a32, oth_ref, cA, ib, rc)
+        corr_tile(cB, kmat_ref, pos_ref, corrx, jnp.maximum(t - 1, 0))
+        cross_tile(a32, oth_ref, cB, ib + 1, rc)
+        corr_tile(cA, kmat_ref, pos_ref, corrx, t)
+        return 0
+
+    lax.fori_loop(0, 16, body, 0)
+    corr_tile(cB, kmat_ref, pos_ref, corrx, 31)
+
+    x, y, z, core = place()
+    make_onehot(pos_ref, oh_ref, (1 - core) * 512, 512)
+    away[...] = jnp.dot(oh_ref[...], corrx[...], preferred_element_type=jnp.float32)
+    pl.semaphore_wait(pltpu.get_barrier_semaphore(), NX * NY + NZ - 1)
+    swap = pltpu.make_async_remote_copy(
+        src_ref=away, dst_ref=came, send_sem=core_sems.at[0], recv_sem=core_sems.at[1],
+        device_id=device(x, y, z, 1 - core), device_id_type=MESH)
+    swap.start()
+    make_onehot(pos_ref, oh_ref, core * 512, 512)
+    keep[...] = jnp.dot(oh_ref[...], corrx[...], preferred_element_type=jnp.float32).reshape(NX * NY, 32, 2 * TL)
+    swap.wait()
+
+    def merge(d, _):
+        v = split_counts(keep[d] + came[pl.ds(pl.multiple_of(d * 32, 32), 32), :])
+        keep[d] = v
+        plane_out[d] = v.astype(jnp.bfloat16)
+        return 0
+
+    lax.fori_loop(0, NX * NY, merge, 0)
+
+    def plane_copy(d):
+        px, py, pz, pc = plane_peer(d)
+        return pltpu.make_async_remote_copy(
+            src_ref=plane_out.at[px * NY + py], dst_ref=plane_in.at[d],
+            send_sem=plane_send.at[d], recv_sem=plane_recv.at[d],
+            device_id=device(px, py, pz, pc), device_id_type=MESH)
+
+    def start_plane(d, _):
+        plane_copy(d).start()
+        return 0
+
+    lax.fori_loop(1, NX * NY, start_plane, 0)
+
+    def take_plane(d, acc):
+        plane_copy(d).wait()
+        return acc + plane_in[d].astype(jnp.float32)
+
+    total = lax.fori_loop(1, NX * NY, take_plane, keep[x * NY + y])
+    for i in range(NZ):
+        line_out[i] = total[2 * i:2 * i + 2]
+
+    def line_copy(d):
+        px, py, pz, pc = line_peer(d)
+        return pltpu.make_async_remote_copy(
+            src_ref=line_out.at[pz], dst_ref=line_in.at[d],
+            send_sem=line_send.at[d], recv_sem=line_recv.at[d],
+            device_id=device(px, py, pz, pc), device_id_type=MESH)
+
+    def start_line(d, _):
+        line_copy(d).start()
+        return 0
+
+    lax.fori_loop(1, NZ, start_line, 0)
+
+    def take_line(d, acc):
+        line_copy(d).wait()
+        return acc + line_in[d]
+
+    out_ref[...] = lax.fori_loop(1, NZ, take_line, line_out[z])
+
+
+def run(own, oth, bins, tab, kmat):
+    vm = lambda s, d: pltpu.VMEM(s, d)
+    dma = pltpu.SemaphoreType.DMA
+    return pl.pallas_call(
+        kernel, out_shape=jax.ShapeDtypeStruct((2, 2 * TL), jnp.float32),
+        in_specs=[pl.BlockSpec(memory_space=pltpu.VMEM)] * 5,
+        out_specs=pl.BlockSpec(memory_space=pltpu.VMEM),
+        scratch_shapes=[
+            vm((4, 8, 16, FP), jnp.float32), vm((256, 1024), jnp.bfloat16), vm((256, 1024), jnp.bfloat16),
+            vm((8192, 256), jnp.bfloat16), vm((32, 256), jnp.int32), vm((512, 8192), jnp.bfloat16),
+            vm((512, 256), jnp.float32), vm((512, 256), jnp.float32), vm((16, 32, 256), jnp.float32),
+            vm((16, 32, 256), jnp.bfloat16), vm((16, 32, 256), jnp.bfloat16),
+            vm((16, 2, 256), jnp.float32), vm((16, 2, 256), jnp.float32),
+            dma((2,)), dma((16,)), dma((16,)), dma((16,)), dma((16,)),
+        ],
+        compiler_params=pltpu.CompilerParams(
+            vmem_limit_bytes=60 * 2**20, collective_id=0, has_side_effects=True),
+    )(own, oth, bins, tab, kmat)
+
+
+def perm_tab(p):
+    core, x, y = (p >> 4) & 1, (p >> 2) & 3, p >> 9
+    z, k = (p >> 5) & 15, p & 3
+    return core * 1024 + x * 256 + y * 64 + z * 4 + k
 
 
 def passed_along(value, axis, by):
@@ -113,11 +240,9 @@
 def shards(spectra, mid_bin, off_bin, owner_slot):
     own = prep(spectra)
     other = jnp.concatenate([passed_along(own, "blk", 1), passed_along(own, "blk", 2)], 0)
-    table = owner_slot.reshape(16, 128)
-    part = run(own, other, prep_idx(mid_bin, off_bin), table, lag_matrix())
-    part = part.reshape(2048, TL)
-    total = lax.psum_scatter(part, ("blk", "grp"), scatter_dimension=0, tiled=True)
-    number = total[:, NL:NL + 1]
+    table = perm_tab(owner_slot).reshape(16, 128)
+    total = run(own, other, prep_idx(mid_bin, off_bin), table, lag_matrix()).reshape(4, TL)
+    number = total[:, NL:NL + 1] + total[:, NL + 1:NL + 2]
     return (total[:, :NL] / jnp.sqrt(jnp.maximum(number, 1.0))).T
 
 

time: 560 us -> 97.2 us (0.17)
  waiting for transfers between devices: 485 us -> 22.1 us
  Pallas kernels: 44.3 us -> 60.3 us
  between operations: 13.5 us -> 0.13 us
    unnamed x2 -> x0, waiting for transfers between devices: 463 us -> none
    pallas_call x1, Pallas kernels: 44.3 us -> 60.3 us  [run(): pl.pallas_call(kernel, out_shape=jax.ShapeDtypeStruct((2, 2 * TL), jnp.fl...]
  transfers between devices with their start and end apart: 3 -> 2, of which waited for: 3 -> 2; matrix products, arithmetic and copies ran while one was open for 0% -> 2% of each run, Pallas kernels for 0% -> 0%
where the time goes in v2:
time: 97.2 us; the launch traced here: 96.9 us
  Pallas kernels  60.3 us (62%)
  waiting for transfers between devices  22.1 us (23%)
  starting transfers between devices  8.48 us (9%)
  local copies, waits for them, and re-layouts  3.35 us (3%)
  other arithmetic  2.54 us (3%)
    pallas_call x1, Pallas kernels, run(): pl.pallas_call(kernel, out_shape=jax.ShapeDtypeStruct((2, 2 * TL), jnp.fl...  60.3 us
    ppermute x2, waiting for transfers between devices, passed_along(): lax.ppermute(value, axis, [(i, (i + by) % size) for i in range(size)])  22.1 us
    ppermute x2, starting transfers between devices, passed_along(): lax.ppermute(value, axis, [(i, (i + by) % size) for i in range(size)])  8.48 us
  transfers between devices with their start and end apart: 2, of which 2 were waited for; matrix products, arithmetic and copies ran while one was open for 2% of the time, Pallas kernels for 0%

profile of v2, /device:TPU:1, one launch (start us, length us, event | category | flops | bytes accessed | tf_op | source)
XLA Modules:
  0.0 96.9 jit_solution(17204566672936943265)
XLA Ops:
  0.0 1.5 %reshape.18 = bf16[4,16,4,2,501]{4,3,2,1,0:T(2,128)(2,1)S(1)} reshape(bf16[64,4,1002]{2,1,0:T(4,128)(2,1)} %param.5) | data formatting | bytes 1026048 | tf_op jit(solution)/shard_map/reshape | solution.py:22
  1.5 0.2 copy.12
  1.7 0.0 copy-start.1
  1.7 0.0 copy-start.2
  1.7 0.1 pad.4
  1.8 0.0 copy-start
  1.8 4.9 %collective-permute-start = (bf16[4,8,16,512]{3,2,1,0:T(8,128)(2,1)S(1)}, bf16[4,8,16,512]{3,2,1,0:T(8,128)(2,1)S(1)}, u32[]{:S(2)}, u32[]{:S(2)}) collective-permute-start(bf16[4,8,16,512]{3,2,1,0:T(8,128)(2,1)S(1)} %bitcast.13), channel_id=1, source_target_pairs={{0,4},{4,8},{8,12},{12,16},{16,20},{20,24},{24,28},{28,32},{32,36}... | collective-permute-start | bytes 1572872 | tf_op jit(solution)/shard_map/ppermute | solution.py:237
  6.7 3.5 %collective-permute-start.1 = (bf16[4,8,16,512]{3,2,1,0:T(8,128)(2,1)S(1)}, bf16[4,8,16,512]{3,2,1,0:T(8,128)(2,1)S(1)}, u32[]{:S(2)}, u32[]{:S(2)}) collective-permute-start(bf16[4,8,16,512]{3,2,1,0:T(8,128)(2,1)S(1)} %bitcast.14), channel_id=1, source_target_pairs={{0,8},{4,12},{8,16},{12,20},{16,24},{20,28},{24,32},{28,36},{32,40... | collective-permute-start | bytes 1572872 | tf_op jit(solution)/shard_map/ppermute | solution.py:237
  10.3 0.0 copy-done.1
  10.3 0.0 copy-done.2
  10.3 0.2 reshape.20
  10.5 0.0 copy-done
  10.5 0.0 copy-start.3
  10.5 0.7 reshape.21.bin_ref
  11.3 0.0 copy-done.3
  11.3 0.6 add_bitcast_fusion.tab_ref
  11.9 0.9 collective-permute-done
  12.8 21.2 %collective-permute-done.1 = bf16[4,8,16,512]{3,2,1,0:T(8,128)(2,1)S(1)} collective-permute-done((bf16[4,8,16,512]{3,2,1,0:T(8,128)(2,1)S(1)}, bf16[4,8,16,512]{3,2,1,0:T(8,128)(2,1)S(1)}, u32[]{:S(2)}, u32[]{:S(2)}) %collective-permute-start.1) | collective-permute-done | bytes 524320 | tf_op jit(solution)/shard_map/ppermute | solution.py:237
  34.0 1.1 %pad_maximum_fusion.oth_ref = bf16[8,8,16,512]{3,2,1,0:T(8,128)(2,1)} fusion(bf16[4,8,16,512]{3,2,1,0:T(8,128)(2,1)S(1)} %collective-permute-done.1, bf16[4,8,16,512]{3,2,1,0:T(8,128)(2,1)S(1)} %collective-permute-done), kind=kLoop, calls=%fused_computation | loop fusion | flops 524288 | bytes 2097152 | tf_op jit(solution)/shard_map/concatenate | solution.py:242
  35.0 60.3 %shard_map.55 = f32[2,256]{1,0:T(2,128)} custom-call(bf16[4,8,16,512]{3,2,1,0:T(8,128)(2,1)} %bitcast.15, bf16[8,8,16,512]{3,2,1,0:T(8,128)(2,1)} %pad_maximum_fusion.oth_ref, s32[32,256]{1,0:T(8,128)} %reshape.21.bin_ref, s32[16,128]{1,0:T(8,128)} %add_bitcast_fusion.tab_ref, bf16[1024,128]{1,0:T(8,128)(2,1)} %constant.29.clone.kmat_ref), custom_call_target="tpu_custom_call" | custom-call | tf_op jit(solution)/shard_map/pallas_call | solution.py:212
  95.4 0.7 reshape.23
  96.1 0.2 sqrt_reduce_fusion
  96.2 0.7 divide_bitcast_fusion
  (2 shorter events, 0.0 us)
Async XLA Ops:
  1.7 8.6 %copy-start.1 = (s32[2,64,64]{2,1,0:T(8,128)S(1)}, s32[2,64,64]{2,1,0:T(8,128)}, u32[]{:S(2)}) copy-start(s32[2,64,64]{2,1,0:T(8,128)} %param.7) | copy-start | bytes 98308
  1.7 8.6 %copy-start.2 = (s32[2,64,64]{2,1,0:T(8,128)S(1)}, s32[2,64,64]{2,1,0:T(8,128)}, u32[]{:S(2)}) copy-start(s32[2,64,64]{2,1,0:T(8,128)} %param.6) | copy-start | bytes 98308
  1.8 8.7 %copy-start = (bf16[4,2,4,16,512]{4,3,2,1,0:T(8,128)(2,1)}, bf16[4,2,4,16,512]{4,3,2,1,0:T(8,128)(2,1)S(1)}, u32[]{:S(2)}) copy-start(bf16[4,2,4,16,512]{4,3,2,1,0:T(8,128)(2,1)S(1)} %pad.4) | copy-start | bytes 1572868
  1.8 11.0 %collective-permute-start = (bf16[4,8,16,512]{3,2,1,0:T(8,128)(2,1)S(1)}, bf16[4,8,16,512]{3,2,1,0:T(8,128)(2,1)S(1)}, u32[]{:S(2)}, u32[]{:S(2)}) collective-permute-start(bf16[4,8,16,512]{3,2,1,0:T(8,128)(2,1)S(1)} %bitcast.13), channel_id=1, source_target_pairs={{0,4},{4,8},{8,12},{12,16},{16,20},{20,24},{24,28},{28,32},{32,36}... | collective-permute-start | bytes 1572872 | tf_op jit(solution)/shard_map/ppermute | solution.py:237
  6.7 27.3 %collective-permute-start.1 = (bf16[4,8,16,512]{3,2,1,0:T(8,128)(2,1)S(1)}, bf16[4,8,16,512]{3,2,1,0:T(8,128)(2,1)S(1)}, u32[]{:S(2)}, u32[]{:S(2)}) collective-permute-start(bf16[4,8,16,512]{3,2,1,0:T(8,128)(2,1)S(1)} %bitcast.14), channel_id=1, source_target_pairs={{0,8},{4,12},{8,16},{12,20},{16,24},{20,28},{24,32},{28,36},{32,40... | collective-permute-start | bytes 1572872 | tf_op jit(solution)/shard_map/ppermute | solution.py:237
  10.5 0.8 copy-start.3

commit v3 on v2

v3 whole, which is shorter than its diff:
```python
import jax
import jax.numpy as jnp
import numpy as np
from jax import lax
from jax.experimental import pallas as pl
from jax.experimental.pallas import tpu as pltpu
from jax.sharding import PartitionSpec as P

LAG = 50
NOFF = 16
F = 501
W = 4
FP = 512
TL = 128
NL = 2 * LAG + 1
bf16, f32 = jnp.bfloat16, jnp.float32


def lag_matrix():
    freq = np.arange(F, dtype=np.float32)
    lags = (np.arange(NL) - LAG).astype(np.float32)
    angle = (np.float32(2.0 * np.pi) * freq[:, None] * lags[None, :] / np.float32(2 * (F - 1))).astype(np.float32)
    w = np.where((freq == 0) | (freq == F - 1), 1.0, 2.0).astype(np.float32) / np.sqrt(np.float32(W * F))
    k = np.zeros((TL, 2 * FP), np.float32)
    k[:NL, :F] = (w[:, None] * np.cos(angle)).T
    k[:NL, FP:FP + F] = (-w[:, None] * np.sin(angle)).T
    return jnp.asarray(k, bf16)


def prep(spectra):
    x = spectra.reshape(64, W, 2, F).transpose(1, 2, 0, 3)
    x = jnp.pad(x, ((0, 0),) * 3 + ((0, FP - F),))
    return x.reshape(8, 64, FP)


def prep_tile(x_ref, bt_ref, ag_ref, q):
    lane = lax.broadcasted_iota(jnp.int32, (64, 128), 1)
    xs = []
    for k in range(8):
        x = x_ref[k, :, pl.ds(q * 128, 128)].astype(f32)
        xs.append(x)
        y = jnp.transpose(jnp.concatenate([x, pltpu.roll(x, 96, 1)], 0)).astype(bf16)
        bt_ref[2 * q, pl.ds(k * 32, 32), :] = y[0:32]
        bt_ref[2 * q + 1, pl.ds(k * 32, 32), :] = y[64:96]
    for s in range(4):
        for h in range(2):
            acc = None
            for m in range(4):
                shift = (32 * (m - s)) % 128
                v = xs[4 * h + m]
                v = pltpu.roll(v, shift, 1) if shift else v
                acc = v if acc is None else jnp.where(lane >= 32 * m, v, acc)
            ag_ref[(4 * q + s) * 2 + h] = acc


def weights(u_ref, v_ref, w_ref, gp, sign):
    lane = lax.broadcasted_iota(jnp.int32, (32, 128), 1)
    left = lane < 64
    sgn = jnp.where(left, 1.0, sign)
    for k in range(8):
        u = u_ref[gp, pl.ds(k * 32, 32), :].astype(f32)
        v = v_ref[gp, pl.ds(k * 32, 32), :].astype(f32)
        ur, vr = pltpu.roll(u, 64, 1), pltpu.roll(v, 64, 1)
        for n, val in ((0, jnp.where(left, u, vr)), (1, jnp.where(left, ur, v))):
            w_ref[n, 0, pl.ds(k * 32, 32), :] = val.astype(bf16)
            other = val * sgn if k % 2 == 0 else -(val * sgn)
            w_ref[n, 1, pl.ds((k ^ 1) * 32, 32), :] = other.astype(bf16)


def stage1(ag_ref, w_ref, ct_ref, gp):
    MI = 8
    row = lax.broadcasted_iota(jnp.int32, (32, 128), 0)
    lane = lax.broadcasted_iota(jnp.int32, (32, 128), 1)
    mask = jnp.where((lane & 31) == row, 1.0, 0.0).astype(bf16)

    def body(ib, _):
        for n in range(2):
            w = jnp.concatenate([w_ref[n, 0], w_ref[n, 1]], 1)
            for h in range(MH):
                parts = []
                for ii in range(MI):
                    halves = []
                    for q in range(2):
                        a = ag_ref[(2 * gp + n) * 2 + q, pl.ds((ib * MH + h) * MI + ii, 1), :]
                        a = jnp.broadcast_to(a, (16, 128)).astype(bf16)
                        halves.append(jnp.concatenate([a, a], 0) * mask)
                    parts.append(jnp.concatenate(halves, 1))
                e = jnp.concatenate(parts, 0)
                o = jnp.dot(e, w, preferred_element_type=f32).astype(bf16)
                r0 = pl.multiple_of((2 * gp + n) * 32, 32)
                for ii in range(MI):
                    p = ((ib * MH + h) * MI + ii) // 2
                    ct_ref[ii % 2, p, pl.ds(r0, 32), :] = o[ii * 32:ii * 32 + 32, 0:128]
                    ct_ref[ii % 2, p, pl.ds(r0 + FP, 32), :] = o[ii * 32:ii * 32 + 32, 128:256]
        return 0

    lax.fori_loop(0, 64 // (MI * MH), body, 0)


MH = 4


def stage2(kt_ref, ct_ref, pos_ref, cx_ref):
    sub = lax.broadcasted_iota(jnp.int32, (TL, 128), 0)
    count = (sub == NL) | (sub == NL + 1)

    def body(s, _):
        for u in range(4):
            ip = 4 * s + u
            w = jnp.concatenate([ct_ref[0, ip], ct_ref[1, ip]], 1)
            c = jnp.dot(kt_ref[...], w, preferred_element_type=f32)
            row = pos_ref[pl.ds(ip, 1), :]
            for h in range(2):
                ch = jnp.where(count, 1.0, c[:, h * 128:h * 128 + 128]).astype(bf16)
                bit = (row[:, h * 128:h * 128 + 128] & 1).astype(f32)
                bit = jnp.broadcast_to(bit, (TL, 128)).astype(bf16)
                hi = ch * bit
                cx_ref[h, ip, pl.ds(0, TL), :] = ch - hi
                cx_ref[h, ip, pl.ds(TL, TL), :] = hi
        return 0

    lax.fori_loop(0, 8, body, 0)


def lookup(bin_ref, tab_ref, pos_ref):
    tab = tab_ref[...]
    tt = jnp.concatenate([(tab & 255).astype(f32), (tab >> 8).astype(f32)], 0).astype(bf16)
    sub = lax.broadcasted_iota(jnp.int32, (128, 256), 0)
    s16 = lax.broadcasted_iota(jnp.int32, (16, 256), 0)

    def body(s, _):
        for u in range(8):
            b = bin_ref[pl.ds(8 * s + u, 1), :]
            oh = jnp.where(sub == (b & 127), 1.0, 0.0).astype(bf16)
            v = jnp.dot(tt, oh, preferred_element_type=f32)
            full = v[:16] + 256.0 * v[16:]
            p = jnp.sum(jnp.where(s16 == (b >> 7), full, 0.0), axis=0, keepdims=True)
            pos_ref[pl.ds(8 * s + u, 1), :] = p.astype(jnp.int32)
        return 0

    lax.fori_loop(0, 4, body, 0)


def binning(pos_ref, cx_ref, acc_ref, base):
    sub = lax.broadcasted_iota(jnp.int32, (256, 128), 0).astype(f32).astype(bf16)
    one, zero = jnp.ones((), bf16), jnp.zeros((), bf16)

    def body(s, _):
        lhs, rhs = [], []
        for u in range(KB):
            t = KB * s + u
            row = pos_ref[pl.ds(t, 1), :]
            for q in range(2):
                a = row[:, q * 128:q * 128 + 128] >> 1
                lo, hi = a & 255, a >> 8
                col = []
                for h in range(2):
                    key = jnp.where(hi == base + h, lo, -1).astype(f32)
                    key = jnp.broadcast_to(key, (256, 128)).astype(bf16)
                    col.append(jnp.where(sub == key, one, zero))
                lhs.append(jnp.concatenate(col, 0))
                rhs.append(cx_ref[q, t])
        o = lax.dot_general(jnp.concatenate(lhs, 1), jnp.concatenate(rhs, 1), (((1,), (1,)), ((), ())), preferred_element_type=f32)
        acc_ref[...] = acc_ref[...] + o
        return 0

    acc_ref[...] = jnp.zeros_like(acc_ref)
    lax.fori_loop(0, 32 // KB, body, 0)


KB = 4


NX, NY, NZ = 4, 4, 16
MESH = pl.DeviceIdType.MESH


def place():
    blk = lax.axis_index("blk")
    return lax.axis_index("grp"), blk // (2 * NZ), lax.rem(blk // 2, NZ), lax.rem(blk, 2)


def device(x, y, z, core):
    return {"blk": (y * NZ + z) * 2 + core, "grp": x}


def plane_peer(d):
    x, y, z, core = place()
    return lax.rem(x + d // NY, NX), lax.rem(y + lax.rem(d, NY), NY), z, core


def line_peer(d):
    x, y, z, core = place()
    return x, y, lax.rem(z + d, NZ), core


def chip_neighbour(by, core):
    n = lax.axis_size("blk")
    chip = lax.axis_index("blk") // 2
    return {"blk": lax.rem(chip + by + n // 2, n // 2) * 2 + core, "grp": lax.axis_index("grp")}


def greet():
    barrier = pltpu.get_barrier_semaphore()
    x, y, z, core = place()

    def tell(device_id):
        pl.semaphore_signal(barrier, inc=1, device_id=device_id, device_id_type=MESH)

    tell(device(x, y, z, 1 - core))
    for by in (1, -1):
        for c in range(2):
            tell(chip_neighbour(by, c))

    def plane(d, _):
        tell(device(*plane_peer(d)))
        return 0

    def line(d, _):
        tell(device(*line_peer(d)))
        return 0

    lax.fori_loop(1, NX * NY, plane, 0)
    lax.fori_loop(1, NZ, line, 0)


def split_counts(v):
    lane = lax.rem(lax.broadcasted_iota(jnp.int32, v.shape, len(v.shape) - 1), TL)
    high = jnp.floor(v * (1.0 / 128.0)) * 128.0
    return jnp.where(lane == NL, high, jnp.where(lane == NL + 1, v - high, v))


def remote(src, dst, send, recv, to):
    return pltpu.make_async_remote_copy(
        src_ref=src, dst_ref=dst, send_sem=send, recv_sem=recv, device_id=to, device_id_type=MESH)


def kernel(x_ref, ubin_ref, vbin_ref, tab_ref, kt_ref, out_ref,
           bt, ag, ub, vb, w, ct, cx, vbin, bins, pos, away, came, keep,
           plane_out, plane_in, line_out, line_in,
           bin_sems, send1, send2, fwd_send, u_recv, v_recv,
           core_sems, plane_send, plane_recv, line_send, line_recv):
    greet()
    x, y, z, core = place()
    sibling = device(x, y, z, 1 - core)
    for q in range(4):
        prep_tile(x_ref, bt, ag, q)
    pl.semaphore_wait(pltpu.get_barrier_semaphore(), NX * NY + NZ + 3)

    def bin_copy():
        return remote(vbin_ref, vbin, bin_sems.at[0], bin_sems.at[1], chip_neighbour(-1, 0))

    def up_copy(g):
        return remote(bt.at[g], ub.at[g], send1.at[g], u_recv.at[g], chip_neighbour(1, lax.rem(g, 2)))

    def side_copy(g):
        return remote(bt.at[g], vb.at[g], send1.at[g], v_recv.at[g], sibling)

    def down_copy(g):
        return remote(bt.at[g], vb.at[g], send2.at[g], v_recv.at[g], chip_neighbour(-1, 0))

    def forward(g):
        return remote(ub.at[g], ub.at[g], fwd_send.at[g], u_recv.at[g], sibling)

    @pl.when(core == 0)
    def _():
        bin_copy().start()

        def start(g, _):
            down_copy(g).start()
            side_copy(g).start()
            return 0

        lax.fori_loop(0, 8, start, 0)
        bin_copy().wait()

    @pl.when(core == 1)
    def _():
        def start(g, _):
            up_copy(g).start()
            return 0

        lax.fori_loop(0, 8, start, 0)
        vbin[...] = vbin_ref[...]

    bins[...] = ubin_ref[...] + vbin[...]
    lookup(bins, tab_ref, pos)
    sign = jnp.where(core == 0, -1.0, 1.0)

    def chunk(s, _):
        first = 2 * (s // 2) + core
        g = jnp.where(lax.rem(s, 2) == 0, first, 4 * (s // 2) + 1 - first)
        forward(g).wait_recv()

        @pl.when(lax.rem(s, 2) == 0)
        def _():
            forward(g).start()

        side_copy(g).wait_recv()
        weights(ub, vb, w, g, sign)
        stage1(ag, w, ct, g)
        return 0

    lax.fori_loop(0, 8, chunk, 0)
    stage2(kt_ref, ct, pos, cx)

    binning(pos, cx, away, 2 * (1 - core))
    swap = remote(away, came, core_sems.at[0], core_sems.at[1], sibling)
    swap.start()
    binning(pos, cx, keep, 2 * core)
    swap.wait()

    def merge(d, _):
        rows = pl.ds(pl.multiple_of(d * 32, 32), 32)
        v = split_counts(keep[rows, :] + came[rows, :])
        keep[rows, :] = v
        plane_out[d] = v.astype(bf16)
        return 0

    lax.fori_loop(0, NX * NY, merge, 0)

    def plane_copy(d):
        px, py, pz, pc = plane_peer(d)
        return remote(plane_out.at[px * NY + py], plane_in.at[d], plane_send.at[d], plane_recv.at[d],
                      device(px, py, pz, pc))

    def start_plane(d, _):
        plane_copy(d).start()
        return 0

    lax.fori_loop(1, NX * NY, start_plane, 0)

    def take_plane(d, acc):
        plane_copy(d).wait()
        return acc + plane_in[d].astype(f32)

    mine = keep[pl.ds(pl.multiple_of((x * NY + y) * 32, 32), 32), :]
    total = lax.fori_loop(1, NX * NY, take_plane, mine)
    for i in range(NZ):
        line_out[i] = total[2 * i:2 * i + 2]

    def line_copy(d):
        px, py, pz, pc = line_peer(d)
        return remote(line_out.at[pz], line_in.at[d], line_send.at[d], line_recv.at[d], device(px, py, pz, pc))

    def start_line(d, _):
        line_copy(d).start()
        return 0

    lax.fori_loop(1, NZ, start_line, 0)

    def take_line(d, acc):
        line_copy(d).wait()
        return acc + line_in[d]

    out_ref[...] = lax.fori_loop(1, NZ, take_line, line_out[z])

    @pl.when(core == 0)
    def _():
        def finish(g, _):
            down_copy(g).wait_send()
            side_copy(g).wait_send()
            return 0

        lax.fori_loop(0, 8, finish, 0)

    @pl.when(core == 1)
    def _():
        def finish(g, _):
            up_copy(g).wait_send()
            return 0

        lax.fori_loop(0, 8, finish, 0)

    def finish(s, _):
        forward(2 * s + core).wait_send()
        return 0

    lax.fori_loop(0, 4, finish, 0)


def run(*args):
    vm = pltpu.VMEM
    dma = pltpu.SemaphoreType.DMA
    i32 = jnp.int32
    return pl.pallas_call(
        kernel, out_shape=jax.ShapeDtypeStruct((2, 2 * TL), f32),
        in_specs=[pl.BlockSpec(memory_space=pltpu.VMEM)] * 5,
        out_specs=pl.BlockSpec(memory_space=pltpu.VMEM),
        scratch_shapes=[
            vm((8, 256, 128), bf16), vm((32, 64, 128), f32), vm((8, 256, 128), bf16), vm((8, 256, 128), bf16),
            vm((2, 2, 256, 128), bf16), vm((2, 32, 1024, 128), bf16), vm((2, 32, 256, 128), bf16),
            vm((32, 256), i32), vm((32, 256), i32), vm((32, 256), i32),
            vm((512, 256), f32), vm((512, 256), f32), vm((512, 256), f32),
            vm((16, 32, 256), bf16), vm((16, 32, 256), bf16), vm((16, 2, 256), f32), vm((16, 2, 256), f32),
            dma((2,)), dma((8,)), dma((8,)), dma((8,)), dma((8,)), dma((8,)),
            dma((2,)), dma((16,)), dma((16,)), dma((16,)), dma((16,)),
        ],
        compiler_params=pltpu.CompilerParams(
            vmem_limit_bytes=60 * 2**20, collective_id=0, has_side_effects=True),
    )(*args)


def perm_tab(p):
    core, x, y = (p >> 4) & 1, (p >> 2) & 3, p >> 9
    z, k = (p >> 5) & 15, p & 3
    return core * 1024 + x * 256 + y * 64 + z * 4 + k


def quarters(b, v):
    b = b.reshape(32, 2, 1, 64)
    pad = jnp.zeros_like(b)
    return jnp.concatenate([pad, b] if v else [b, pad], 2).reshape(32, 256)


def shards(spectra, mid_bin, off_bin, owner_slot):
    b = mid_bin * NOFF + off_bin
    upper = lax.rem(lax.axis_index("blk"), 2) == 1
    ubin = quarters(jnp.where(upper, b[1], b[0]), False)
    vbin = quarters(jnp.where(upper, b[0], b[1].T), True)
    table = perm_tab(owner_slot).reshape(16, 128)
    total = run(prep(spectra), ubin, vbin, table, lag_matrix()).reshape(4, TL)
    number = total[:, NL:NL + 1] + total[:, NL + 1:NL + 2]
    return (total[:, :NL] / jnp.sqrt(jnp.maximum(number, 1.0))).T


def solution(mesh):
    in_specs = (
        P(("blk", "grp"), None, None),
        P(None, ("blk", "grp"), None),
        P(None, ("blk", "grp"), None),
        P(),
    )
    return jax.shard_map(shards, mesh=mesh, in_specs=in_specs, out_specs=P(None, ("blk", "grp")), check_vma=False)
```

time: 97.2 us -> 64.6 us (0.66)
  waiting for transfers between devices: 22.1 us -> 0 us
  starting transfers between devices: 8.48 us -> 0 us
  Pallas kernels: 60.3 us -> 57 us
  local copies, waits for them, and re-layouts: 3.35 us -> 5.76 us
  other arithmetic: 2.54 us -> 1.48 us
    ppermute x2 -> x0, waiting for transfers between devices: 22.1 us -> none  [passed_along(): lax.ppermute(value, axis, [(i, (i + by) % size) for i in range(size)])]
    ppermute x2 -> x0, starting transfers between devices: 8.48 us -> none  [passed_along(): lax.ppermute(value, axis, [(i, (i + by) % size) for i in range(size)])]
    pallas_call x1, Pallas kernels: 60.3 us -> 57 us  [run(): pl.pallas_call(kernel, out_shape=jax.ShapeDtypeStruct((2, 2 * TL), f32),...]
    concatenate x1 -> x0, other arithmetic: 1.06 us -> none  [shards(): jnp.concatenate([passed_along(own, 'blk', 1), passed_along(own, 'blk', 2)...]
    unnamed x8 -> x9, local copies, waits for them, and re-layouts: 0.02 us -> 1 us
    reshape x6 -> x5, local copies, waits for them, and re-layouts: 3.27 us -> 3.78 us  [the longest x2 1.65 us: prep(): x = spectra.reshape(64, W, 2, F).transpose(1, 2, 0, 3)]
  transfers between devices with their start and end apart: 2 -> 0, of which waited for: 2 -> 0; matrix products, arithmetic and copies ran while one was open for 2% -> 0% of each run, Pallas kernels for 0% -> 0%
where the time goes in v3:
time: 64.6 us; the launch traced here: 64.3 us
  Pallas kernels  57 us (88%)
  local copies, waits for them, and re-layouts  5.76 us (9%)
  other arithmetic  1.48 us (2%)
    pallas_call x1, Pallas kernels, run(): pl.pallas_call(kernel, out_shape=jax.ShapeDtypeStruct((2, 2 * TL), f32),...  57 us
    reshape x2, local copies, waits for them, and re-layouts, prep(): x = spectra.reshape(64, W, 2, F).transpose(1, 2, 0, 3)  1.65 us
    reshape x2, local copies, waits for them, and re-layouts, quarters(): return jnp.concatenate([pad, b] if v else [b, pad], 2).reshape(32, 256)  1.44 us

profile of v3, /device:TPU:1, one launch (start us, length us, event | category | flops | bytes accessed | tf_op | source)
XLA Modules:
  0.0 64.3 jit_solution(8004761847465995248)
XLA Ops:
  0.0 1.5 %reshape.41 = bf16[64,4,2,501]{3,2,1,0:T(2,128)(2,1)S(1)} reshape(bf16[64,4,1002]{2,1,0:T(4,128)(2,1)} %param.5) | data formatting | bytes 1026048 | tf_op jit(solution)/shard_map/reshape | solution.py:31
  1.5 0.2 copy.21
  1.7 0.0 copy-start
  1.7 0.8 %pad.6 = bf16[4,2,64,512]{3,2,1,0:T(8,128)(2,1)} pad(bf16[4,2,64,501]{3,2,1,0:T(8,128)(2,1)S(1)} %bitcast.21, bf16[]{:T(256)} %constant.17.clone.1), padding=0_0x0_0x0_0x0_11 | pad | bytes 1037314 | tf_op jit(solution)/shard_map/jit(_pad)/pad | solution.py:32
  2.5 0.0 copy-done
  2.5 0.0 copy-start.1
  2.5 0.1 copy.13
  2.6 0.8 %copy-done.1 = s32[2,64,64]{2,1,0:T(8,128)S(1)} copy-done((s32[2,64,64]{2,1,0:T(8,128)S(1)}, s32[2,64,64]{2,1,0:T(8,128)}, u32[]{:S(2)}) %copy-start.1) | copy-done | bytes 32792
  3.4 0.1 copy.12
  3.5 0.1 copy.15
  3.5 0.1 copy.18
  3.7 0.7 %reshape.43.ubin_ref = s32[32,256]{1,0:T(8,128)} reshape(s32[32,2,2,64]{3,2,1,0:T(2,128)S(1)} %concatenate.6.clone) | data formatting | bytes 65536 | tf_op jit(solution)/shard_map/reshape | solution.py:413
  4.5 0.0 copy-start.2
  4.5 0.7 %reshape.45.vbin_ref = s32[32,256]{1,0:T(8,128)} reshape(s32[32,2,2,64]{3,2,1,0:T(2,128)S(1)} %concatenate.7) | data formatting | bytes 65536 | tf_op jit(solution)/shard_map/reshape | solution.py:413
  5.2 0.0 copy-done.2
  5.2 0.6 add_bitcast_fusion.tab_ref
  5.8 57.0 %shard_map.55 = f32[2,256]{1,0:T(2,128)} custom-call(bf16[8,64,512]{2,1,0:T(8,128)(2,1)} %bitcast.20, s32[32,256]{1,0:T(8,128)} %reshape.43.ubin_ref, s32[32,256]{1,0:T(8,128)} %reshape.45.vbin_ref, s32[16,128]{1,0:T(8,128)} %add_bitcast_fusion.tab_ref, bf16[128,1024]{1,0:T(8,128)(2,1)} %constant.41.clone.kt_ref), custom_call_target="tpu_custom_call" | custom-call | tf_op jit(solution)/shard_map/pallas_call | solution.py:386
  62.8 0.7 %reshape.47 = f32[4,128]{1,0:T(4,128)S(1)} reshape(f32[2,256]{1,0:T(2,128)} %shard_map.55) | data formatting | bytes 4096 | tf_op jit(solution)/shard_map/reshape | solution.py:422
  63.5 0.2 sqrt_reduce_fusion
  63.7 0.7 %divide_bitcast_fusion = f32[101,4]{0,1:T(4,128)} fusion(f32[4,128]{1,0:T(4,128)S(1)} %reshape.47, f32[4]{0:T(128)S(1)} %sqrt_reduce_fusion), kind=kLoop, calls=%fused_computation.5 | loop fusion | flops 404 | bytes 3248 | tf_op jit(solution)/shard_map/transpose | solution.py:424
  (6 shorter events, 0.1 us)
Async XLA Ops:
  1.7 0.8 %copy-start = (s32[2,64,64]{2,1,0:T(8,128)S(1)}, s32[2,64,64]{2,1,0:T(8,128)}, u32[]{:S(2)}) copy-start(s32[2,64,64]{2,1,0:T(8,128)} %param.7) | copy-start | bytes 98308
  2.5 0.8 %copy-start.1 = (s32[2,64,64]{2,1,0:T(8,128)S(1)}, s32[2,64,64]{2,1,0:T(8,128)}, u32[]{:S(2)}) copy-start(s32[2,64,64]{2,1,0:T(8,128)} %param.6) | copy-start | bytes 98308
  4.5 0.7 %copy-start.2 = (s32[2048]{0:T(1024)S(1)}, s32[2048]{0:T(1024)}, u32[]{:S(2)}) copy-start(s32[2048]{0:T(1024)} %param.8) | copy-start | bytes 24580

commit v4 on v3

--- a/solution.py
+++ b/solution.py
@@ -27,18 +27,36 @@
     return jnp.asarray(k, bf16)
 
 
-def prep(spectra):
-    x = spectra.reshape(64, W, 2, F).transpose(1, 2, 0, 3)
-    x = jnp.pad(x, ((0, 0),) * 3 + ((0, FP - F),))
-    return x.reshape(8, 64, FP)
-
-
-def prep_tile(x_ref, bt_ref, ag_ref, q):
+def spread(x_ref, rows_ref):
+    for i in range(64):
+        x = x_ref[i].astype(f32)
+        for t in range(8):
+            n = min(128, 2 * F - 128 * t)
+            rows_ref[t, pl.ds(8 * i, W), pl.ds(0, n)] = x[:, 128 * t:128 * t + n]
+
+
+def parts(rows_ref, q):
     lane = lax.broadcasted_iota(jnp.int32, (64, 128), 1)
-    xs = []
+    cut = F - FP + 128
+    gap = FP - F
+    out = []
+    for w in range(W):
+        def tile(t):
+            return rows_ref[t, pl.ds(w, 64, stride=8), :]
+
+        re = tile(q)
+        im = jnp.where(lane < gap, pltpu.roll(tile(q + 3), gap, 1), pltpu.roll(tile(q + 4), gap, 1))
+        if q == 3:
+            re, im = jnp.where(lane < cut, re, 0.0), jnp.where(lane < cut, im, 0.0)
+        out += [re, im]
+    return out
+
+
+def prep_tile(rows_ref, bt_ref, ag_ref, q):
+    lane = lax.broadcasted_iota(jnp.int32, (64, 128), 1)
+    xs = parts(rows_ref, q)
     for k in range(8):
-        x = x_ref[k, :, pl.ds(q * 128, 128)].astype(f32)
-        xs.append(x)
+        x = xs[k]
         y = jnp.transpose(jnp.concatenate([x, pltpu.roll(x, 96, 1)], 0)).astype(bf16)
         bt_ref[2 * q, pl.ds(k * 32, 32), :] = y[0:32]
         bt_ref[2 * q + 1, pl.ds(k * 32, 32), :] = y[64:96]
@@ -109,10 +127,10 @@
             ip = 4 * s + u
             w = jnp.concatenate([ct_ref[0, ip], ct_ref[1, ip]], 1)
             c = jnp.dot(kt_ref[...], w, preferred_element_type=f32)
-            row = pos_ref[pl.ds(ip, 1), :]
             for h in range(2):
+                row = pos_ref[pl.ds(2 * ip + h, 1), :]
                 ch = jnp.where(count, 1.0, c[:, h * 128:h * 128 + 128]).astype(bf16)
-                bit = (row[:, h * 128:h * 128 + 128] & 1).astype(f32)
+                bit = (row & 1).astype(f32)
                 bit = jnp.broadcast_to(bit, (TL, 128)).astype(bf16)
                 hi = ch * bit
                 cx_ref[h, ip, pl.ds(0, TL), :] = ch - hi
@@ -122,23 +140,40 @@
     lax.fori_loop(0, 8, body, 0)
 
 
-def lookup(bin_ref, tab_ref, pos_ref):
-    tab = tab_ref[...]
+def lookup(slot_ref, tab_ref, bins_ref, pos_ref):
+    for r in range(16):
+        tab_ref[pl.ds(r, 1), :] = slot_ref[pl.ds(128 * r, 128)].reshape(1, 128)
+    p = tab_ref[...]
+    core, x, y = (p >> 4) & 1, (p >> 2) & 3, p >> 9
+    z, k = (p >> 5) & 15, p & 3
+    tab = core * 1024 + x * 256 + y * 64 + z * 4 + k
     tt = jnp.concatenate([(tab & 255).astype(f32), (tab >> 8).astype(f32)], 0).astype(bf16)
     sub = lax.broadcasted_iota(jnp.int32, (128, 256), 0)
     s16 = lax.broadcasted_iota(jnp.int32, (16, 256), 0)
 
     def body(s, _):
         for u in range(8):
-            b = bin_ref[pl.ds(8 * s + u, 1), :]
+            t = 16 * s + 2 * u
+            b = jnp.concatenate([bins_ref[pl.ds(t, 1), :], bins_ref[pl.ds(t + 1, 1), :]], 1)
             oh = jnp.where(sub == (b & 127), 1.0, 0.0).astype(bf16)
             v = jnp.dot(tt, oh, preferred_element_type=f32)
             full = v[:16] + 256.0 * v[16:]
-            p = jnp.sum(jnp.where(s16 == (b >> 7), full, 0.0), axis=0, keepdims=True)
-            pos_ref[pl.ds(8 * s + u, 1), :] = p.astype(jnp.int32)
+            p = jnp.sum(jnp.where(s16 == (b >> 7), full, 0.0), axis=0, keepdims=True).astype(jnp.int32)
+            pos_ref[pl.ds(t, 1), :] = p[:, :128]
+            pos_ref[pl.ds(t + 1, 1), :] = p[:, 128:]
         return 0
 
     lax.fori_loop(0, 4, body, 0)
+
+
+def pair_bins(mid_ref, off_ref, upper, s0, s1, ubin, vbin):
+    s0[...] = jnp.zeros_like(s0)
+    s1[...] = jnp.zeros_like(s1)
+    s0[:, pl.ds(0, 64)] = (mid_ref[0] * NOFF + off_ref[0]).astype(f32)
+    s1[pl.ds(0, 64), pl.ds(0, 64)] = (mid_ref[1] * NOFF + off_ref[1]).astype(f32)
+    near, far = s0[...], s1[...]
+    ubin[...] = jnp.where(upper, far[0:64], near).astype(jnp.int32)
+    vbin[...] = pltpu.roll(jnp.where(upper, near, jnp.transpose(far)[0:64]), 64, 1).astype(jnp.int32)
 
 
 def binning(pos_ref, cx_ref, acc_ref, base):
@@ -149,9 +184,8 @@
         lhs, rhs = [], []
         for u in range(KB):
             t = KB * s + u
-            row = pos_ref[pl.ds(t, 1), :]
             for q in range(2):
-                a = row[:, q * 128:q * 128 + 128] >> 1
+                a = pos_ref[pl.ds(2 * t + q, 1), :] >> 1
                 lo, hi = a & 255, a >> 8
                 col = []
                 for h in range(2):
@@ -171,6 +205,15 @@
 KB = 4
 
 
+def finish(total, fin, out_ref):
+    for r in range(2):
+        for h in range(2):
+            fin[pl.ds(2 * r + h, 1), :] = total[r:r + 1, h * TL:h * TL + TL]
+    t = fin[0:4, :]
+    number = t[:, NL:NL + 1] + t[:, NL + 1:NL + 2]
+    out_ref[...] = t[:, :NL] / jnp.sqrt(jnp.maximum(number, 1.0))
+
+
 NX, NY, NZ = 4, 4, 16
 MESH = pl.DeviceIdType.MESH
 
@@ -235,20 +278,22 @@
         src_ref=src, dst_ref=dst, send_sem=send, recv_sem=recv, device_id=to, device_id_type=MESH)
 
 
-def kernel(x_ref, ubin_ref, vbin_ref, tab_ref, kt_ref, out_ref,
-           bt, ag, ub, vb, w, ct, cx, vbin, bins, pos, away, came, keep,
+def kernel(x_ref, mid_ref, off_ref, slot_ref, kt_ref, out_ref,
+           rows, tab, s0, s1, fin, bt, ag, ub, vb, w, ct, cx, ubin, vbin, vin, pos, away, came, keep,
            plane_out, plane_in, line_out, line_in,
            bin_sems, send1, send2, fwd_send, u_recv, v_recv,
            core_sems, plane_send, plane_recv, line_send, line_recv):
     greet()
     x, y, z, core = place()
     sibling = device(x, y, z, 1 - core)
+    spread(x_ref, rows)
     for q in range(4):
-        prep_tile(x_ref, bt, ag, q)
+        prep_tile(rows, bt, ag, q)
+    pair_bins(mid_ref, off_ref, core == 1, s0, s1, ubin, vbin)
     pl.semaphore_wait(pltpu.get_barrier_semaphore(), NX * NY + NZ + 3)
 
     def bin_copy():
-        return remote(vbin_ref, vbin, bin_sems.at[0], bin_sems.at[1], chip_neighbour(-1, 0))
+        return remote(vbin, vin, bin_sems.at[0], bin_sems.at[1], chip_neighbour(-1, 0))
 
     def up_copy(g):
         return remote(bt.at[g], ub.at[g], send1.at[g], u_recv.at[g], chip_neighbour(1, lax.rem(g, 2)))
@@ -281,10 +326,10 @@
             return 0
 
         lax.fori_loop(0, 8, start, 0)
-        vbin[...] = vbin_ref[...]
-
-    bins[...] = ubin_ref[...] + vbin[...]
-    lookup(bins, tab_ref, pos)
+        vin[...] = vbin[...]
+
+    ubin[...] = ubin[...] + vin[...]
+    lookup(slot_ref, tab, ubin, pos)
     sign = jnp.where(core == 0, -1.0, 1.0)
 
     def chunk(s, _):
@@ -311,9 +356,9 @@
     swap.wait()
 
     def merge(d, _):
-        rows = pl.ds(pl.multiple_of(d * 32, 32), 32)
-        v = split_counts(keep[rows, :] + came[rows, :])
-        keep[rows, :] = v
+        at = pl.ds(pl.multiple_of(d * 32, 32), 32)
+        v = split_counts(keep[at, :] + came[at, :])
+        keep[at, :] = v
         plane_out[d] = v.astype(bf16)
         return 0
 
@@ -353,30 +398,30 @@
         line_copy(d).wait()
         return acc + line_in[d]
 
-    out_ref[...] = lax.fori_loop(1, NZ, take_line, line_out[z])
+    finish(lax.fori_loop(1, NZ, take_line, line_out[z]), fin, out_ref)
 
     @pl.when(core == 0)
     def _():
-        def finish(g, _):
+        def drain(g, _):
             down_copy(g).wait_send()
             side_copy(g).wait_send()
             return 0
 
-        lax.fori_loop(0, 8, finish, 0)
+        lax.fori_loop(0, 8, drain, 0)
 
     @pl.when(core == 1)
     def _():
-        def finish(g, _):
+        def drain(g, _):
             up_copy(g).wait_send()
             return 0
 
-        lax.fori_loop(0, 8, finish, 0)
-
-    def finish(s, _):
+        lax.fori_loop(0, 8, drain, 0)
+
+    def drain(s, _):
         forward(2 * s + core).wait_send()
         return 0
 
-    lax.fori_loop(0, 4, finish, 0)
+    lax.fori_loop(0, 4, drain, 0)
 
 
 def run(*args):
@@ -384,13 +429,14 @@
     dma = pltpu.SemaphoreType.DMA
     i32 = jnp.int32
     return pl.pallas_call(
-        kernel, out_shape=jax.ShapeDtypeStruct((2, 2 * TL), f32),
+        kernel, out_shape=jax.ShapeDtypeStruct((4, NL), f32),
         in_specs=[pl.BlockSpec(memory_space=pltpu.VMEM)] * 5,
         out_specs=pl.BlockSpec(memory_space=pltpu.VMEM),
         scratch_shapes=[
+            vm((8, 512, 128), f32), vm((16, 128), i32), vm((64, 128), f32), vm((128, 128), f32), vm((8, 128), f32),
             vm((8, 256, 128), bf16), vm((32, 64, 128), f32), vm((8, 256, 128), bf16), vm((8, 256, 128), bf16),
             vm((2, 2, 256, 128), bf16), vm((2, 32, 1024, 128), bf16), vm((2, 32, 256, 128), bf16),
-            vm((32, 256), i32), vm((32, 256), i32), vm((32, 256), i32),
+            vm((64, 128), i32), vm((64, 128), i32), vm((64, 128), i32), vm((64, 128), i32),
             vm((512, 256), f32), vm((512, 256), f32), vm((512, 256), f32),
             vm((16, 32, 256), bf16), vm((16, 32, 256), bf16), vm((16, 2, 256), f32), vm((16, 2, 256), f32),
             dma((2,)), dma((8,)), dma((8,)), dma((8,)), dma((8,)), dma((8,)),
@@ -401,27 +447,8 @@
     )(*args)
 
 
-def perm_tab(p):
-    core, x, y = (p >> 4) & 1, (p >> 2) & 3, p >> 9
-    z, k = (p >> 5) & 15, p & 3
-    return core * 1024 + x * 256 + y * 64 + z * 4 + k
-
-
-def quarters(b, v):
-    b = b.reshape(32, 2, 1, 64)
-    pad = jnp.zeros_like(b)
-    return jnp.concatenate([pad, b] if v else [b, pad], 2).reshape(32, 256)
-
-
 def shards(spectra, mid_bin, off_bin, owner_slot):
-    b = mid_bin * NOFF + off_bin
-    upper = lax.rem(lax.axis_index("blk"), 2) == 1
-    ubin = quarters(jnp.where(upper, b[1], b[0]), False)
-    vbin = quarters(jnp.where(upper, b[0], b[1].T), True)
-    table = perm_tab(owner_slot).reshape(16, 128)
-    total = run(prep(spectra), ubin, vbin, table, lag_matrix()).reshape(4, TL)
-    number = total[:, NL:NL + 1] + total[:, NL + 1:NL + 2]
-    return (total[:, :NL] / jnp.sqrt(jnp.maximum(number, 1.0))).T
+    return run(spectra, mid_bin, off_bin, owner_slot, lag_matrix()).T
 
 
 def solution(mesh):

time: 64.6 us -> 58.6 us (0.907)
  local copies, waits for them, and re-layouts: 5.76 us -> 1.26 us
  other arithmetic: 1.48 us -> 0 us
    reshape x5 -> x0, local copies, waits for them, and re-layouts: 3.78 us -> none  [the longest x2 1.65 us: prep(): x = spectra.reshape(64, W, 2, F).transpose(1, 2, 0, 3)]
    pad x1 -> x0, local copies, waits for them, and re-layouts: 0.83 us -> none  [prep(): x = jnp.pad(x, ((0, 0),) * 3 + ((0, FP - F),))]
    transpose x1 -> x0, other arithmetic: 0.67 us -> none  [shards(): return (total[:, :NL] / jnp.sqrt(jnp.maximum(number, 1.0))).T]
where the time goes in v4:
time: 58.6 us; the launch traced here: 58.5 us
  Pallas kernels  57.2 us (98%)
  local copies, waits for them, and re-layouts  1.26 us (2%)
    pallas_call x1, Pallas kernels, run(): pl.pallas_call(kernel, out_shape=jax.ShapeDtypeStruct((4, NL), f32), in_s...  57.2 us
    unnamed x1, local copies, waits for them, and re-layouts  1.26 us

profile of v4, /device:TPU:1, one launch (start us, length us, event | category | flops | bytes accessed | tf_op | source)
XLA Modules:
  0.0 58.5 jit_solution(15273149387472697681)
XLA Ops:
  0.0 57.2 %shard_map.55 = f32[4,101]{1,0:T(4,128)} custom-call(bf16[64,4,1002]{2,1,0:T(4,128)(2,1)} %x_ref.1, s32[2,64,64]{2,1,0:T(8,128)} %mid_ref.1, s32[2,64,64]{2,1,0:T(8,128)} %off_ref.1, s32[2048]{0:T(1024)} %slot_ref.1, bf16[128,1024]{1,0:T(8,128)(2,1)} %constant.2.clone.kt_ref), custom_call_target="tpu_custom_call" | custom-call | tf_op jit(solution)/shard_map/pallas_call | solution.py:431
  57.2 1.3 %copy.7 = f32[101,4]{0,1:T(4,128)} copy(f32[101,4]{0,1:T(4,128)} %bitcast.1) | data formatting | bytes 3232

commit v5 on v4

--- a/solution.py
+++ b/solution.py
@@ -86,7 +86,7 @@
 
 
 def stage1(ag_ref, w_ref, ct_ref, gp):
-    MI = 8
+    MI = 16
     row = lax.broadcasted_iota(jnp.int32, (32, 128), 0)
     lane = lax.broadcasted_iota(jnp.int32, (32, 128), 1)
     mask = jnp.where((lane & 31) == row, 1.0, 0.0).astype(bf16)
@@ -123,8 +123,8 @@
     count = (sub == NL) | (sub == NL + 1)
 
     def body(s, _):
-        for u in range(4):
-            ip = 4 * s + u
+        for u in range(8):
+            ip = 8 * s + u
             w = jnp.concatenate([ct_ref[0, ip], ct_ref[1, ip]], 1)
             c = jnp.dot(kt_ref[...], w, preferred_element_type=f32)
             for h in range(2):
@@ -137,7 +137,7 @@
                 cx_ref[h, ip, pl.ds(TL, TL), :] = hi
         return 0
 
-    lax.fori_loop(0, 8, body, 0)
+    lax.fori_loop(0, 4, body, 0)
 
 
 def lookup(slot_ref, tab_ref, bins_ref, pos_ref):
@@ -177,6 +177,7 @@
 
 
 def binning(pos_ref, cx_ref, acc_ref, base):
+    n = acc_ref.shape[0] // 256
     sub = lax.broadcasted_iota(jnp.int32, (256, 128), 0).astype(f32).astype(bf16)
     one, zero = jnp.ones((), bf16), jnp.zeros((), bf16)
 
@@ -188,7 +189,7 @@
                 a = pos_ref[pl.ds(2 * t + q, 1), :] >> 1
                 lo, hi = a & 255, a >> 8
                 col = []
-                for h in range(2):
+                for h in range(n):
                     key = jnp.where(hi == base + h, lo, -1).astype(f32)
                     key = jnp.broadcast_to(key, (256, 128)).astype(bf16)
                     col.append(jnp.where(sub == key, one, zero))
@@ -202,16 +203,16 @@
     lax.fori_loop(0, 32 // KB, body, 0)
 
 
-KB = 4
-
-
-def finish(total, fin, out_ref):
+KB = 16
+
+
+def finish(total, out_ref):
     for r in range(2):
         for h in range(2):
-            fin[pl.ds(2 * r + h, 1), :] = total[r:r + 1, h * TL:h * TL + TL]
-    t = fin[0:4, :]
+            out_ref[pl.ds(2 * r + h, 1), :] = total[r:r + 1, h * TL:h * TL + TL]
+    t = out_ref[...]
     number = t[:, NL:NL + 1] + t[:, NL + 1:NL + 2]
-    out_ref[...] = t[:, :NL] / jnp.sqrt(jnp.maximum(number, 1.0))
+    out_ref[...] = t / jnp.sqrt(jnp.maximum(number, 1.0))
 
 
 NX, NY, NZ = 4, 4, 16
@@ -278,8 +279,12 @@
         src_ref=src, dst_ref=dst, send_sem=send, recv_sem=recv, device_id=to, device_id_type=MESH)
 
 
+def hops(d, size):
+    return min(d, size - d)
+
+
 def kernel(x_ref, mid_ref, off_ref, slot_ref, kt_ref, out_ref,
-           rows, tab, s0, s1, fin, bt, ag, ub, vb, w, ct, cx, ubin, vbin, vin, pos, away, came, keep,
+           rows, tab, s0, s1, bt, ag, ub, vb, w, ct, cx, ubin, vbin, vin, pos, away, came, keep,
            plane_out, plane_in, line_out, line_in,
            bin_sems, send1, send2, fwd_send, u_recv, v_recv,
            core_sems, plane_send, plane_recv, line_send, line_recv):
@@ -352,8 +357,11 @@
     binning(pos, cx, away, 2 * (1 - core))
     swap = remote(away, came, core_sems.at[0], core_sems.at[1], sibling)
     swap.start()
-    binning(pos, cx, keep, 2 * core)
-    swap.wait()
+
+    def plane_copy(d):
+        px, py, pz, pc = plane_peer(d)
+        return remote(plane_out.at[px * NY + py], plane_in.at[d], plane_send.at[d], plane_recv.at[d],
+                      device(px, py, pz, pc))
 
     def merge(d, _):
         at = pl.ds(pl.multiple_of(d * 32, 32), 32)
@@ -362,18 +370,16 @@
         plane_out[d] = v.astype(bf16)
         return 0
 
-    lax.fori_loop(0, NX * NY, merge, 0)
-
-    def plane_copy(d):
-        px, py, pz, pc = plane_peer(d)
-        return remote(plane_out.at[px * NY + py], plane_in.at[d], plane_send.at[d], plane_recv.at[d],
-                      device(px, py, pz, pc))
-
-    def start_plane(d, _):
-        plane_copy(d).start()
-        return 0
-
-    lax.fori_loop(1, NX * NY, start_plane, 0)
+    far_first = sorted(range(1, NX * NY), key=lambda d: -hops(d // NY, NX) - hops(d % NY, NY))
+    for piece in range(2):
+        binning(pos, cx, keep.at[pl.ds(256 * piece, 256)], 2 * core + piece)
+        if piece == 0:
+            swap.wait()
+        lax.fori_loop(8 * piece, 8 * piece + 8, merge, 0)
+        for d in far_first:
+            @pl.when(plane_peer(d)[0] // 2 == piece)
+            def _():
+                plane_copy(d).start()
 
     def take_plane(d, acc):
         plane_copy(d).wait()
@@ -388,17 +394,14 @@
         px, py, pz, pc = line_peer(d)
         return remote(line_out.at[pz], line_in.at[d], line_send.at[d], line_recv.at[d], device(px, py, pz, pc))
 
-    def start_line(d, _):
+    for d in sorted(range(1, NZ), key=lambda d: -hops(d, NZ)):
         line_copy(d).start()
-        return 0
-
-    lax.fori_loop(1, NZ, start_line, 0)
 
     def take_line(d, acc):
         line_copy(d).wait()
         return acc + line_in[d]
 
-    finish(lax.fori_loop(1, NZ, take_line, line_out[z]), fin, out_ref)
+    finish(lax.fori_loop(1, NZ, take_line, line_out[z]), out_ref)
 
     @pl.when(core == 0)
     def _():
@@ -429,11 +432,11 @@
     dma = pltpu.SemaphoreType.DMA
     i32 = jnp.int32
     return pl.pallas_call(
-        kernel, out_shape=jax.ShapeDtypeStruct((4, NL), f32),
+        kernel, out_shape=jax.ShapeDtypeStruct((4, TL), f32),
         in_specs=[pl.BlockSpec(memory_space=pltpu.VMEM)] * 5,
         out_specs=pl.BlockSpec(memory_space=pltpu.VMEM),
         scratch_shapes=[
-            vm((8, 512, 128), f32), vm((16, 128), i32), vm((64, 128), f32), vm((128, 128), f32), vm((8, 128), f32),
+            vm((8, 512, 128), f32), vm((16, 128), i32), vm((64, 128), f32), vm((128, 128), f32),
             vm((8, 256, 128), bf16), vm((32, 64, 128), f32), vm((8, 256, 128), bf16), vm((8, 256, 128), bf16),
             vm((2, 2, 256, 128), bf16), vm((2, 32, 1024, 128), bf16), vm((2, 32, 256, 128), bf16),
             vm((64, 128), i32), vm((64, 128), i32), vm((64, 128), i32), vm((64, 128), i32),
@@ -448,7 +451,7 @@
 
 
 def shards(spectra, mid_bin, off_bin, owner_slot):
-    return run(spectra, mid_bin, off_bin, owner_slot, lag_matrix()).T
+    return run(spectra, mid_bin, off_bin, owner_slot, lag_matrix())[:, :NL].T
 
 
 def solution(mesh):

time: 58.6 us -> 52.2 us (0.89)
  Pallas kernels: 57.2 us -> 50.4 us
    pallas_call x1, Pallas kernels: 57.2 us -> 50.4 us  [run(): pl.pallas_call(kernel, out_shape=jax.ShapeDtypeStruct((4, TL), f32), in_s...]
    transpose x0 -> x1, local copies, waits for them, and re-layouts: none -> 1.26 us  [shards(): return run(spectra, mid_bin, off_bin, owner_slot, lag_matrix())[:, :NL].T]
    unnamed x1 -> x0, local copies, waits for them, and re-layouts: 1.26 us -> none
where the time goes in v5:
time: 52.2 us; the launch traced here: 51.7 us
  Pallas kernels  50.4 us (97%)
  local copies, waits for them, and re-layouts  1.26 us (2%)
    pallas_call x1, Pallas kernels, run(): pl.pallas_call(kernel, out_shape=jax.ShapeDtypeStruct((4, TL), f32), in_s...  50.4 us
    transpose x1, local copies, waits for them, and re-layouts, shards(): return run(spectra, mid_bin, off_bin, owner_slot, lag_matrix())[:, :NL].T  1.26 us

profile of v5, /device:TPU:1, one launch (start us, length us, event | category | flops | bytes accessed | tf_op | source)
XLA Modules:
  0.0 51.7 jit_solution(11592278923510279757)
XLA Ops:
  0.0 50.4 %shard_map.55 = f32[4,128]{1,0:T(4,128)} custom-call(bf16[64,4,1002]{2,1,0:T(4,128)(2,1)} %x_ref.1, s32[2,64,64]{2,1,0:T(8,128)} %mid_ref.1, s32[2,64,64]{2,1,0:T(8,128)} %off_ref.1, s32[2048]{0:T(1024)} %slot_ref.1, bf16[128,1024]{1,0:T(8,128)(2,1)} %constant.2.clone.kt_ref), custom_call_target="tpu_custom_call" | custom-call | tf_op jit(solution)/shard_map/pallas_call | solution.py:434
  50.4 1.3 %slice_bitcast_fusion = f32[101,4]{0,1:T(4,128)} fusion(f32[4,128]{1,0:T(4,128)} %shard_map.55), kind=kLoop, calls=%fused_computation | loop fusion | bytes 3232 | tf_op jit(solution)/shard_map/transpose | solution.py:454

commit v6 on v5

--- a/solution.py
+++ b/solution.py
@@ -244,28 +244,23 @@
     return {"blk": lax.rem(chip + by + n // 2, n // 2) * 2 + core, "grp": lax.axis_index("grp")}
 
 
+def torus_neighbours():
+    x, y, z, core = place()
+    for by in (1, -1):
+        yield device(lax.rem(x + by + NX, NX), y, z, core)
+        yield device(x, lax.rem(y + by + NY, NY), z, core)
+        yield device(x, y, lax.rem(z + by + NZ, NZ), core)
+
+
 def greet():
     barrier = pltpu.get_barrier_semaphore()
     x, y, z, core = place()
-
-    def tell(device_id):
+    near = [device(x, y, z, 1 - core)]
+    near += [chip_neighbour(by, c) for by in (1, -1) for c in range(2)]
+    near += list(torus_neighbours())
+    for device_id in near:
         pl.semaphore_signal(barrier, inc=1, device_id=device_id, device_id_type=MESH)
-
-    tell(device(x, y, z, 1 - core))
-    for by in (1, -1):
-        for c in range(2):
-            tell(chip_neighbour(by, c))
-
-    def plane(d, _):
-        tell(device(*plane_peer(d)))
-        return 0
-
-    def line(d, _):
-        tell(device(*line_peer(d)))
-        return 0
-
-    lax.fori_loop(1, NX * NY, plane, 0)
-    lax.fori_loop(1, NZ, line, 0)
+    return len(near)
 
 
 def split_counts(v):
@@ -287,15 +282,14 @@
            rows, tab, s0, s1, bt, ag, ub, vb, w, ct, cx, ubin, vbin, vin, pos, away, came, keep,
            plane_out, plane_in, line_out, line_in,
            bin_sems, send1, send2, fwd_send, u_recv, v_recv,
-           core_sems, plane_send, plane_recv, line_send, line_recv):
-    greet()
+           rounds, core_sems, plane_send, plane_recv, line_send, line_recv):
+    near = greet()
     x, y, z, core = place()
     sibling = device(x, y, z, 1 - core)
     spread(x_ref, rows)
-    for q in range(4):
-        prep_tile(rows, bt, ag, q)
+    prep_tile(rows, bt, ag, 0)
     pair_bins(mid_ref, off_ref, core == 1, s0, s1, ubin, vbin)
-    pl.semaphore_wait(pltpu.get_barrier_semaphore(), NX * NY + NZ + 3)
+    pl.semaphore_wait(pltpu.get_barrier_semaphore(), near)
 
     def bin_copy():
         return remote(vbin, vin, bin_sems.at[0], bin_sems.at[1], chip_neighbour(-1, 0))
@@ -316,21 +310,27 @@
     def _():
         bin_copy().start()
 
-        def start(g, _):
-            down_copy(g).start()
-            side_copy(g).start()
-            return 0
-
-        lax.fori_loop(0, 8, start, 0)
+    for q in range(4):
+        if q > 0:
+            prep_tile(rows, bt, ag, q)
+
+        @pl.when(core == 0)
+        def _():
+            for g in (2 * q, 2 * q + 1):
+                down_copy(g).start()
+                side_copy(g).start()
+
+        @pl.when(core == 1)
+        def _():
+            for g in (2 * q, 2 * q + 1):
+                up_copy(g).start()
+
+    @pl.when(core == 0)
+    def _():
         bin_copy().wait()
 
     @pl.when(core == 1)
     def _():
-        def start(g, _):
-            up_copy(g).start()
-            return 0
-
-        lax.fori_loop(0, 8, start, 0)
         vin[...] = vbin[...]
 
     ubin[...] = ubin[...] + vin[...]
@@ -349,14 +349,34 @@
         side_copy(g).wait_recv()
         weights(ub, vb, w, g, sign)
         stage1(ag, w, ct, g)
-        return 0
-
+
+        @pl.when(lax.rem(s, 3) == 2)
+        def _():
+            hear(s // 3)
+            spread_word(s // 3 + 1)
+
+        return 0
+
+    def spread_word(r):
+        for device_id in torus_neighbours():
+            pl.semaphore_signal(rounds.at[r], inc=1, device_id=device_id, device_id_type=MESH)
+
+    def hear(r):
+        pl.semaphore_wait(rounds.at[r], 6)
+
+    spread_word(0)
     lax.fori_loop(0, 8, chunk, 0)
+    hear(2)
+    spread_word(3)
     stage2(kt_ref, ct, pos, cx)
+    hear(3)
+    spread_word(4)
 
     binning(pos, cx, away, 2 * (1 - core))
     swap = remote(away, came, core_sems.at[0], core_sems.at[1], sibling)
     swap.start()
+    hear(4)
+    spread_word(5)
 
     def plane_copy(d):
         px, py, pz, pc = plane_peer(d)
@@ -372,14 +392,20 @@
 
     far_first = sorted(range(1, NX * NY), key=lambda d: -hops(d // NY, NX) - hops(d % NY, NY))
     for piece in range(2):
-        binning(pos, cx, keep.at[pl.ds(256 * piece, 256)], 2 * core + piece)
+        half = 1 - x // 2 if piece == 0 else x // 2
+        at = pl.multiple_of(256 * half, 256)
+        binning(pos, cx, keep.at[pl.ds(at, 256)], 2 * core + half)
         if piece == 0:
             swap.wait()
-        lax.fori_loop(8 * piece, 8 * piece + 8, merge, 0)
+        lax.fori_loop(8 * half, 8 * half + 8, merge, 0)
         for d in far_first:
-            @pl.when(plane_peer(d)[0] // 2 == piece)
+            @pl.when(plane_peer(d)[0] // 2 == half)
             def _():
                 plane_copy(d).start()
+
+        if piece == 0:
+            hear(5)
+            spread_word(6)
 
     def take_plane(d, acc):
         plane_copy(d).wait()
@@ -394,6 +420,7 @@
         px, py, pz, pc = line_peer(d)
         return remote(line_out.at[pz], line_in.at[d], line_send.at[d], line_recv.at[d], device(px, py, pz, pc))
 
+    hear(6)
     for d in sorted(range(1, NZ), key=lambda d: -hops(d, NZ)):
         line_copy(d).start()
 
@@ -443,6 +470,7 @@
             vm((512, 256), f32), vm((512, 256), f32), vm((512, 256), f32),
             vm((16, 32, 256), bf16), vm((16, 32, 256), bf16), vm((16, 2, 256), f32), vm((16, 2, 256), f32),
             dma((2,)), dma((8,)), dma((8,)), dma((8,)), dma((8,)), dma((8,)),
+            pltpu.SemaphoreType.REGULAR((NZ // 2 - 1,)),
             dma((2,)), dma((16,)), dma((16,)), dma((16,)), dma((16,)),
         ],
         compiler_params=pltpu.CompilerParams(

time: 52.2 us -> 50.8 us (0.973)
  Pallas kernels: 50.4 us -> 49.4 us
    pallas_call x1, Pallas kernels: 50.4 us -> 49.4 us  [run(): pl.pallas_call(kernel, out_shape=jax.ShapeDtypeStruct((4, TL), f32), in_s...]
where the time goes in v6:
time: 50.8 us; the launch traced here: 50.6 us
  Pallas kernels  49.4 us (97%)
  local copies, waits for them, and re-layouts  1.26 us (2%)
    pallas_call x1, Pallas kernels, run(): pl.pallas_call(kernel, out_shape=jax.ShapeDtypeStruct((4, TL), f32), in_s...  49.4 us
    transpose x1, local copies, waits for them, and re-layouts, shards(): return run(spectra, mid_bin, off_bin, owner_slot, lag_matrix())[:, :NL].T  1.26 us

profile of v6, /device:TPU:1, one launch (start us, length us, event | category | flops | bytes accessed | tf_op | source)
XLA Modules:
  0.0 50.6 jit_solution(5322890854911948787)
XLA Ops:
  0.0 49.4 %shard_map.55 = f32[4,128]{1,0:T(4,128)} custom-call(bf16[64,4,1002]{2,1,0:T(4,128)(2,1)} %x_ref.1, s32[2,64,64]{2,1,0:T(8,128)} %mid_ref.1, s32[2,64,64]{2,1,0:T(8,128)} %off_ref.1, s32[2048]{0:T(1024)} %slot_ref.1, bf16[128,1024]{1,0:T(8,128)(2,1)} %constant.2.clone.kt_ref), custom_call_target="tpu_custom_call" | custom-call | tf_op jit(solution)/shard_map/pallas_call | solution.py:461
  49.4 1.3 %slice_bitcast_fusion = f32[101,4]{0,1:T(4,128)} fusion(f32[4,128]{1,0:T(4,128)} %shard_map.55), kind=kLoop, calls=%fused_computation | loop fusion | bytes 3232 | tf_op jit(solution)/shard_map/transpose | solution.py:482

commit v7 on v6

--- a/solution.py
+++ b/solution.py
@@ -372,9 +372,21 @@
     hear(3)
     spread_word(4)
 
-    binning(pos, cx, away, 2 * (1 - core))
-    swap = remote(away, came, core_sems.at[0], core_sems.at[1], sibling)
-    swap.start()
+    def half_of(piece):
+        return lax.rem(1 - x // 2 + piece, 2)
+
+    def swap(piece):
+        at = pl.ds(pl.multiple_of(256 * half_of(piece), 256), 256)
+        return remote(away.at[at], came.at[at], core_sems.at[piece], core_sems.at[2 + piece], sibling)
+
+    def give(piece, _):
+        half = half_of(piece)
+        at = pl.multiple_of(256 * half, 256)
+        binning(pos, cx, away.at[pl.ds(at, 256)], 2 * (1 - core) + half)
+        swap(piece).start()
+        return 0
+
+    lax.fori_loop(0, 2, give, 0)
     hear(4)
     spread_word(5)
 
@@ -392,11 +404,10 @@
 
     far_first = sorted(range(1, NX * NY), key=lambda d: -hops(d // NY, NX) - hops(d % NY, NY))
     for piece in range(2):
-        half = 1 - x // 2 if piece == 0 else x // 2
+        half = half_of(piece)
         at = pl.multiple_of(256 * half, 256)
         binning(pos, cx, keep.at[pl.ds(at, 256)], 2 * core + half)
-        if piece == 0:
-            swap.wait()
+        swap(piece).wait()
         lax.fori_loop(8 * half, 8 * half + 8, merge, 0)
         for d in far_first:
             @pl.when(plane_peer(d)[0] // 2 == half)
@@ -471,7 +482,7 @@
             vm((16, 32, 256), bf16), vm((16, 32, 256), bf16), vm((16, 2, 256), f32), vm((16, 2, 256), f32),
             dma((2,)), dma((8,)), dma((8,)), dma((8,)), dma((8,)), dma((8,)),
             pltpu.SemaphoreType.REGULAR((NZ // 2 - 1,)),
-            dma((2,)), dma((16,)), dma((16,)), dma((16,)), dma((16,)),
+            dma((4,)), dma((16,)), dma((16,)), dma((16,)), dma((16,)),
         ],
         compiler_params=pltpu.CompilerParams(
             vmem_limit_bytes=60 * 2**20, collective_id=0, has_side_effects=True),

time: 50.8 us -> 50.9 us (level)
  no operation moved by 1% of the time
where the time goes in v7:
time: 50.9 us; the launch traced here: 50.7 us
  Pallas kernels  49.5 us (97%)
  local copies, waits for them, and re-layouts  1.26 us (2%)
    pallas_call x1, Pallas kernels, run(): pl.pallas_call(kernel, out_shape=jax.ShapeDtypeStruct((4, TL), f32), in_s...  49.5 us
    transpose x1, local copies, waits for them, and re-layouts, shards(): return run(spectra, mid_bin, off_bin, owner_slot, lag_matrix())[:, :NL].T  1.26 us

profile of v7, /device:TPU:1, one launch (start us, length us, event | category | flops | bytes accessed | tf_op | source)
XLA Modules:
  0.0 50.7 jit_solution(13760811083072516937)
XLA Ops:
  0.0 49.5 %shard_map.55 = f32[4,128]{1,0:T(4,128)} custom-call(bf16[64,4,1002]{2,1,0:T(4,128)(2,1)} %x_ref.1, s32[2,64,64]{2,1,0:T(8,128)} %mid_ref.1, s32[2,64,64]{2,1,0:T(8,128)} %off_ref.1, s32[2048]{0:T(1024)} %slot_ref.1, bf16[128,1024]{1,0:T(8,128)(2,1)} %constant.2.clone.kt_ref), custom_call_target="tpu_custom_call" | custom-call | tf_op jit(solution)/shard_map/pallas_call | solution.py:472
  49.5 1.3 %slice_bitcast_fusion = f32[101,4]{0,1:T(4,128)} fusion(f32[4,128]{1,0:T(4,128)} %shard_map.55), kind=kLoop, calls=%fused_computation | loop fusion | bytes 3232 | tf_op jit(solution)/shard_map/transpose | solution.py:493
